TPU v7x, 32 devices: a whole 2x2x4 slice. The times are simulated.
32 devices in a mesh: seq: 8 (over z, x), head: 4 (over y, core).
Axes of the slice: x: 2, y: 2, z: 4, core: 2. Of those that a mesh axis runs over, the one named last changes fastest.
Arguments:
- tokens_in: bfloat16 [256, 32, 6144], P('seq', None, 'head'), may hold values from -6 to 6
- gate_rows: bfloat16 [256, 32, 6144], P('seq', None, 'head'), may hold values from -28 to 28
- gate_cols: bfloat16 [256, 32, 6144], P(None, 'seq', 'head'), may hold values from -28 to 28
- write_rows: bfloat16 [64, 8192], P(None, 'seq'), may hold values from -6 to 6
- read_rows: bfloat16 [64, 8192], P(None, 'seq'), may hold values from -0.75 to 0.75
- step_rows: float32 [48, 8192], P('head', 'seq'), may hold values from 0 to 2, as said below
- decay_rows: float32 [48, 8192], P('head', 'seq'), may hold values from -1 to 0, as said below
- skip_rows: float32 [48], P('head'), may hold values from 0.5 to 2
- norm_rows: float32 [6144], P('head'), may hold values from 0.5 to 1.5
- write_cols: bfloat16 [64, 8192], P(None, 'seq'), may hold values from -6 to 6
- read_cols: bfloat16 [64, 8192], P(None, 'seq'), may hold values from -0.75 to 0.75
- step_cols: float32 [48, 8192], P('head', 'seq'), may hold values from 0 to 2, as said below
- decay_cols: float32 [48, 8192], P('head', 'seq'), may hold values from -1 to 0, as said below
- skip_cols: float32 [48], P('head'), may hold values from 0.5 to 2
- norm_cols: float32 [6144], P('head'), may hold values from 0.5 to 1.5
Outputs:
- mixed_cols: bfloat16 [256, 32, 6144], P(None, 'seq', 'head')
Inputs may be any that keep to these rules, and one draw needn't show every extreme that they name: `step_rows`: positive. `step_cols`: positive. `decay_rows`: never positive. `decay_cols`: never positive.
All inputs are finite; a program needn't handle non-finite values.
Results may differ from a plain program's by a relative error of at most 0.0063.
Values may be sent and summed in bfloat16 or wider, within the bound.
A program may use at most 128 MiB of HBM per device.

v0:
```python
import jax
import jax.numpy as jnp
from jax import lax
from jax.sharding import PartitionSpec as P

BLOCK = 256


EPSILON = 1e-05
HIGHEST = lax.Precision.HIGHEST


def carried_state(device_total, end_state):
    totals = lax.all_gather(device_total[None], "seq", axis=0, tiled=True)
    members = totals.shape[0]
    my_index = lax.axis_index("seq")
    source = lax.broadcasted_iota(jnp.int32, (members, members), 0)
    middle = lax.broadcasted_iota(jnp.int32, (members, members), 1)
    between = (source < middle) & (middle < my_index)
    log_spans = jnp.sum(jnp.where(between[:, :, None], totals[None, :, :], 0.0), axis=1)
    earlier = lax.broadcasted_iota(jnp.int32, (members, 1), 0) < my_index
    factors = jnp.where(earlier, jnp.exp(jnp.where(earlier, log_spans, 0.0)), 0.0)
    return jnp.einsum(
        "kh,khnp->hnp",
        factors,
        lax.all_gather(end_state[None], "seq", axis=0, tiled=True),
        precision=HIGHEST,
    )


def ssd_layer(inputs, write_mat, read_mat, step_mat, decay_mat, skip_vec, gain_vec, gate_mat):
    length = inputs.shape[1]
    head_count = inputs.shape[3]
    head_width = inputs.shape[4]
    state_size = write_mat.shape[0]
    col_count = write_mat.shape[1]
    block_count = write_mat.shape[2]
    rows_iota = lax.broadcasted_iota(jnp.int32, (length, length), 0)
    cols_iota = lax.broadcasted_iota(jnp.int32, (length, length), 1)
    upper_ones = (rows_iota <= cols_iota).astype(jnp.float32)
    causal = rows_iota >= cols_iota
    cumulative = jnp.einsum("hcqs,st->hcqt", decay_mat, upper_ones, precision=HIGHEST)
    scores = jnp.einsum("ncqt,ncqs->cqts", read_mat, write_mat, preferred_element_type=jnp.float32)
    spread = cumulative[..., :, None] - cumulative[..., None, :]
    fading = jnp.where(causal, jnp.exp(jnp.where(causal, spread, 0.0)), 0.0)
    mixing = (fading * scores[None] * step_mat[..., None, :]).astype(jnp.bfloat16)
    inner_part = jnp.einsum(
        "hcqts,qschp->qtchp", mixing, inputs, preferred_element_type=jnp.float32
    )
    finals = cumulative[..., -1:]
    tail_weights = jnp.exp(finals - cumulative) * step_mat
    loaded = (write_mat[None] * tail_weights[:, None]).astype(jnp.bfloat16)
    block_states = jnp.einsum(
        "hncqs,qschp->cqhnp", loaded, inputs, preferred_element_type=jnp.float32
    )
    total_blocks = col_count * block_count
    flat_states = block_states.reshape(total_blocks, head_count, state_size, head_width)
    flat_totals = jnp.transpose(finals[..., 0], (1, 2, 0)).reshape(total_blocks, head_count)

    def advance(running, block_item):
        state_now, decay_sum = running
        block_total, block_state = block_item
        moved = (
            jnp.exp(block_total)[:, None, None] * state_now + block_state,
            decay_sum + block_total,
        )
        return (moved, (state_now, decay_sum))

    zero_state = jnp.zeros((head_count, state_size, head_width), jnp.float32)
    zero_total = jnp.zeros((head_count,), jnp.float32)
    scanned = lax.scan(advance, (zero_state, zero_total), (flat_totals, flat_states))
    end_state, device_total = scanned[0]
    incoming, before = scanned[1]
    prior_state = carried_state(device_total, end_state)
    incoming = incoming + jnp.exp(before)[:, :, None, None] * prior_state[None]
    incoming = incoming.reshape(col_count, block_count, head_count, state_size, head_width)
    from_state = jnp.einsum(
        "ncqt,cqhnp->qtchp", read_mat.astype(jnp.float32), incoming, precision=HIGHEST
    )
    lifting = jnp.transpose(jnp.exp(cumulative), (2, 3, 1, 0))[..., None]
    outputs = inner_part + from_state * lifting + skip_vec[:, None] * inputs
    features = gate_mat.shape[-1]
    gated = outputs.reshape(block_count, length, col_count, features) * jax.nn.silu(
        gate_mat.astype(jnp.float32)
    )
    squares = lax.psum(jnp.sum(gated * gated, axis=-1), "head")
    scaled = lax.rsqrt(squares / (features * lax.axis_size("head")) + EPSILON)
    return (gated * scaled[..., None] * gain_vec).astype(jnp.bfloat16)


def body(
    tokens_in,
    gate_rows,
    gate_cols,
    write_rows,
    read_rows,
    step_rows,
    decay_rows,
    skip_rows,
    norm_rows,
    write_cols,
    read_cols,
    step_cols,
    decay_cols,
    skip_cols,
    norm_cols,
):
    grid_rows = tokens_in.shape[0]
    grid_cols = tokens_in.shape[1]
    features = tokens_in.shape[2]
    head_count = step_rows.shape[0]
    head_width = features // head_count
    state_size = write_rows.shape[0]
    tokens = grid_rows * grid_cols
    first_blocks = tokens // BLOCK
    first_out = ssd_layer(
        tokens_in.reshape(first_blocks, BLOCK, 1, head_count, head_width),
        write_rows.reshape(state_size, 1, first_blocks, BLOCK),
        read_rows.reshape(state_size, 1, first_blocks, BLOCK),
        step_rows.reshape(head_count, 1, first_blocks, BLOCK),
        decay_rows.reshape(head_count, 1, first_blocks, BLOCK),
        skip_rows,
        norm_rows,
        gate_rows.reshape(first_blocks, BLOCK, 1, features),
    )
    hidden = lax.all_to_all(
        first_out.reshape(grid_rows, grid_cols, features),
        "seq",
        split_axis=1,
        concat_axis=0,
        tiled=True,
    )
    column_len = hidden.shape[0]
    local_cols = hidden.shape[1]
    col_blocks = column_len // BLOCK
    second_out = ssd_layer(
        hidden.reshape(col_blocks, BLOCK, local_cols, head_count, head_width),
        write_cols.reshape(state_size, local_cols, col_blocks, BLOCK),
        read_cols.reshape(state_size, local_cols, col_blocks, BLOCK),
        step_cols.reshape(head_count, local_cols, col_blocks, BLOCK),
        decay_cols.reshape(head_count, local_cols, col_blocks, BLOCK),
        skip_cols,
        norm_cols,
        gate_cols.reshape(col_blocks, BLOCK, local_cols, features),
    )
    return second_out.reshape(column_len, local_cols, features)


def solution(mesh):
    placed = (
        P("seq", None, "head"),
        P("seq", None, "head"),
        P(None, "seq", "head"),
        P(None, "seq"),
        P(None, "seq"),
        P("head", "seq"),
        P("head", "seq"),
        P("head"),
        P("head"),
        P(None, "seq"),
        P(None, "seq"),
        P("head", "seq"),
        P("head", "seq"),
        P("head"),
        P("head"),
    )
    return jax.shard_map(
        body, mesh=mesh, in_specs=placed, out_specs=P(None, "seq", "head"), check_vma=False
    )
```

profile of v0, /device:TPU:0, one launch (start us, length us, event | category | flops | bytes accessed | tf_op | source)
XLA Modules:
  0.0 353.5 jit_solution(7200968616877671104)
XLA Ops:
  6.5 0.9 reshape.341
  7.4 0.2 fusion.54
  7.8 0.9 mul.274
  8.7 6.9 %reshape.344 = bf16[4,256,12,128]{3,2,1,0:T(8,128)(2,1)} reshape(bf16[32,32,1536]{2,1,0:T(8,128)(2,1)} %param.19) | data formatting | bytes 6291456 | tf_op jit(solution)/shard_map/reshape.13
  15.7 0.7 exponential_multiply_fusion.1
  16.4 4.4 %fusion.37 = f32[4,12,64,128]{3,2,1,0:T(8,128)} fusion(bf16[4,256,12,128]{3,2,1,0:T(8,128)(2,1)} %reshape.344, f32[12,4,256]{2,0,1:T(8,128)S(1)} %get-tuple-element.181, f32[64,4,256]{2,0,1:T(8,128)S(1)} %copy.79), kind=kOutput, calls=%fused_computation.58 | convolution fusion | flops 202899456 | bytes 5029888 | tf_op jit(solution)/shard_map/hncqs,qschp->cqhnp/dot_general | solution.py:53
  20.8 1.3 broadcast.186.clone
  22.2 7.8 %while.34 = (s32[]{:T(128)}, f32[12,64,128]{2,1,0:T(8,128)S(1)}, f32[12]{0:T(128)S(1)}, f32[4,12,64,128]{3,2,1,0:T(8,128)}, f32[4,12]{1,0:T(4,128)S(1)}, /*index...) while((s32[]{:T(128)}, f32[12,64,128]{2,1,0:T(8,128)S(1)}, ...), condition=%wide.region_1.2_spmd.clone, body=%wide.region_0.1_spmd.clone.sunk | while | flops 393243 | bytes 1966593 | solution.py:71
  22.2 0.8 bitcast_dynamic-update-slice_fusion.4
  23.0 1.1 bitcast_add_fusion.4
  24.1 0.8 bitcast_dynamic-update-slice_fusion.4
  24.9 1.1 bitcast_add_fusion.4
  26.1 0.8 bitcast_dynamic-update-slice_fusion.4
  26.9 1.1 bitcast_add_fusion.4
  28.0 0.8 bitcast_dynamic-update-slice_fusion.4
  28.8 1.1 bitcast_add_fusion.4
  30.0 0.8 copy-done.1
  30.7 4.3 %reshape.353 = f32[4,256,1,12,128]{4,3,1,0,2:T(8,128)} reshape(bf16[32,32,1536]{2,1,0:T(8,128)(2,1)S(1)} %copy-done.2) | data formatting | bytes 9437184 | tf_op jit(solution)/shard_map/convert_element_type | solution.py:81
  35.0 7.4 %reshape.354 = f32[4,256,1,12,128]{4,3,1,0,2:T(8,128)} reshape(bf16[32,32,1536]{2,1,0:T(8,128)(2,1)} %param.20) | data formatting | bytes 9437184 | tf_op jit(solution)/shard_map/convert_element_type | solution.py:84
  42.4 9.2 %copy.86 = f32[4,256,1,12,128]{1,4,3,0,2:T(8,128)} copy(f32[4,256,1,12,128]{4,3,1,0,2:T(8,128)} %reshape.354) | data formatting | bytes 12582912 | tf_op jit(solution)/shard_map/convert_element_type | solution.py:84
  51.6 9.2 %copy.83 = f32[4,256,1,12,128]{1,4,3,0,2:T(8,128)} copy(f32[4,256,1,12,128]{4,3,1,0,2:T(8,128)} %reshape.353) | data formatting | bytes 12582912 | tf_op jit(solution)/shard_map/convert_element_type | solution.py:81
  60.9 0.6 dynamic-slice
  62.1 0.2 dynamic-update-slice
  62.3 24.2 %all-reduce = f32[96]{0:T(128)S(1)} all-reduce(f32[96]{0:T(128)S(1)} %dynamic-update-slice), channel_id=2, replica_groups=mesh['seq'=8,'head'=4] {'seq'}, use_global_device_ids=true, to_apply=%add | all-reduce | flops 96 | bytes 768
  87.0 0.3 fusion.61
  87.3 0.2 copy-done.18
  87.6 9.4 %fusion.8 = f32[4,12,256,128]{2,3,1,0:T(8,128)} fusion(f32[12,4,256]{2,0,1:T(8,128)S(1)} %copy-done.16, f32[4,256,256]{2,1,0:T(8,128)S(1)} %fusion.61, f32[12,4,256]{2,0,1:T(8,128)S(1)} %bitcast.164, pred[256,256]{1,0:T(8,128)(4,1)S(1)} %iota_compare_fusion.1, bf16[4,256,12,128]{3,2,1,0:T(8,128)(2,1)} %reshape.344), kind=kOutput, calls=%fused_computation.20 | convolution fusion | flops 824180736 | bytes 10649600 | tf_op jit(solution)/shard_map/hcqts,qschp->qtchp/dot_general | solution.py:47
  97.0 6.2 %fusion.31 = f32[12,1,64,128]{3,1,2,0:T(1,128)S(1)} fusion(f32[8,12,1,1]{0,2,3,1:T(1,128)S(1)} %copy.100, f32[8,12,64,128]{3,2,1,0:T(8,128)} %bitcast.153), kind=kOutput, calls=%fused_computation.49 | convolution fusion | flops 9437184 | bytes 3539328 | tf_op jit(solution)/shard_map/kh,khnp->hnp/dot_general | solution.py:23
  103.3 12.0 %multiply_reduce_fusion.1 = (f32[4,256]{1,0:T(4,128)S(1)}, f32[4,256,1,12,128]{1,4,3,0,2:T(8,128)}) fusion(f32[4,256,1,12,128]{1,4,3,0,2:T(8,128)} %copy.86, f32[4,256,1,12,128]{1,4,3,0,2:T(8,128)} %copy.83, f32[12]{0:T(128)S(1)} %copy-done.27, f32[4,256,12]{1,2,0:T(8,128)S(1)} %copy-done.15, bf16[64,4,256,1]{2,1,0,3:T(4,128)(2,1)S(1)} %bitcast.167, ...), kind=kOutput, calls=%fused_computation.38 | convolution fusion | flops 1226046464 | bytes 27316464 | tf_op jit(solution)/shard_map/ncqt,cqhnp->qtchp/dot_general | solution.py:77
  115.2 9.4 %copy.84 = f32[4,256,1,12,128]{4,3,1,0,2:T(8,128)} copy(f32[4,256,1,12,128]{1,4,3,0,2:T(8,128)} %get-tuple-element.186) | data formatting | bytes 12582912 | tf_op jit(solution)/shard_map/add | solution.py:81
  124.6 8.9 %reshape.346 = f32[32,32,1536]{2,1,0:T(8,128)} reshape(f32[4,256,1,12,128]{4,3,1,0,2:T(8,128)} %copy.84) | data formatting | bytes 12582912 | tf_op jit(solution)/shard_map/reshape | solution.py:83
  133.5 5.8 %psum.14 = f32[4,256,1]{1,0,2:T(4,128)S(1)} all-reduce(f32[4,256,1]{1,0,2:T(4,128)S(1)} %bitcast.170), channel_id=1, replica_groups=mesh['seq'=8,'head'=4] {'head'}, use_global_device_ids=true, to_apply=%region_4.5 | all-reduce | flops 1024 | bytes 8192 | tf_op jit(solution)/shard_map/psum | solution.py:86
  139.5 4.5 %multiply_convert_fusion.5 = bf16[32,32,1536]{2,1,0:T(8,128)(2,1)S(1)} fusion(f32[32,32,1536]{2,1,0:T(8,128)} %reshape.346, f32[1536]{0:T(1024)S(1)} %copy-done.20, f32[32,32]{1,0:T(8,128)S(1)} %mul.294, bf16[32,32,1536]{2,1,0:T(8,128)(2,1)S(1)} %copy-done.4), kind=kLoop, calls=%fused_computation.37 | loop fusion | flops 14155776 | bytes 12593152 | tf_op jit(solution)/shard_map/convert_element_type | solution.py:88
  143.9 3.4 copy.87
  147.3 3.7 %all-to-all-start = ((bf16[32,32,1536]{2,0,1:T(8,128)(2,1)}), bf16[32,32,1536]{2,0,1:T(8,128)(2,1)S(1)}, u32[]{:S(2)}, u32[]{:S(2)}) async-start(bf16[32,32,1536]{2,0,1:T(8,128)(2,1)} %copy.87), calls=%async_computation | async-start | bytes 6291456 | tf_op jit(solution)/shard_map/all_to_all | solution.py:126
  151.1 1.5 reshape.348
  152.5 1.5 mul.301
  154.0 1.6 reshape.350
  155.6 1.6 copy.94
  157.3 1.0 fusion.52
  158.4 0.5 copy-done.13
  158.9 1.5 exponential_multiply_fusion
  160.5 61.5 %all-to-all-done = bf16[32,32,1536]{2,0,1:T(8,128)(2,1)S(1)} async-done(((bf16[32,32,1536]{2,0,1:T(8,128)(2,1)}), bf16[32,32,1536]{2,0,1:T(8,128)(2,1)S(1)}, u32[]{:S(2)}, u32[]{:S(2)}) %all-to-all-start) | async-done | bytes 3145760 | tf_op jit(solution)/shard_map/all_to_all | solution.py:126
  222.0 1.7 copy-done.3
  223.6 5.6 %fusion.73 = (f32[8,32,4,1536]{3,1,0,2:T(8,128)}, bf16[8,32,4,1536]{3,1,0,2:T(8,128)(2,1)S(1)}) fusion(bf16[32,8,4,1536]{3,0,2,1:T(8,128)(2,1)} %bitcast.152), kind=kLoop, calls=%fused_computation.108 | loop fusion | flops 1572864 | bytes 12582912 | tf_op jit(solution)/shard_map/convert_element_type | solution.py:81
  229.2 3.6 %reshape.347 = bf16[256,4,12,128]{3,2,0,1:T(8,128)(2,1)} reshape(bf16[8,32,4,1536]{3,1,0,2:T(8,128)(2,1)S(1)} %get-tuple-element.178) | data formatting | bytes 6291456 | tf_op jit(solution)/shard_map/reshape.66
  232.8 3.4 fusion.34
  236.2 0.2 broadcast.186
  236.4 0.9 while.35
  237.3 0.7 copy-done
  238.0 1.0 reshape.349
  239.0 1.3 fusion.56
  240.3 8.5 %reshape.355 = f32[1,256,4,12,128]{4,3,1,2,0:T(8,128)} reshape(f32[8,32,4,1536]{3,1,0,2:T(8,128)} %get-tuple-element.177) | data formatting | bytes 12582912 | tf_op jit(solution)/shard_map/convert_element_type | solution.py:81
  248.8 9.2 %copy.98 = f32[1,256,4,12,128]{1,4,3,2,0:T(8,128)} copy(f32[1,256,4,12,128]{4,3,1,2,0:T(8,128)} %reshape.355) | data formatting | bytes 12582912 | tf_op jit(solution)/shard_map/convert_element_type | solution.py:81
  258.0 0.2 dynamic-update-slice.1
  258.2 20.3 %all-reduce.1 = f32[96]{0:T(128)S(1)} all-reduce(f32[96]{0:T(128)S(1)} %dynamic-update-slice.1), channel_id=4, replica_groups=mesh['seq'=8,'head'=4] {'seq'}, use_global_device_ids=true, to_apply=%add.1 | all-reduce | flops 96 | bytes 768
  278.9 9.1 %fusion.9 = f32[4,12,128,256]{3,2,1,0:T(8,128)} fusion(f32[12,4,256]{2,0,1:T(8,128)S(1)} %copy-done.17, f32[4,256,256]{2,1,0:T(8,128)S(1)} %fusion.56, f32[12,4,256]{2,0,1:T(8,128)S(1)} %bitcast.166, pred[256,256]{1,0:T(8,128)(4,1)S(1)} %copy-done.19, bf16[256,4,12,128]{3,2,0,1:T(8,128)(2,1)} %reshape.347), kind=kOutput, calls=%fused_computation.21 | convolution fusion | flops 824180736 | bytes 10649600 | tf_op jit(solution)/shard_map/hcqts,qschp->qtchp/dot_general | solution.py:47
  288.0 9.4 %all-gather.9.cloned.1.call-done = f32[96,64,128]{2,1,0:T(8,128)} async-done(((f32[12,64,128]{2,1,0:T(8,128)}), f32[96,64,128]{2,1,0:T(8,128)}) %all-gather.9.cloned.1.call-update) | async-done | bytes 3145744 | tf_op jit(solution)/shard_map/all_gather | solution.py:26
  297.4 6.2 %fusion.29 = f32[12,1,64,128]{3,1,2,0:T(1,128)S(1)} fusion(f32[8,12,1,1]{0,2,3,1:T(1,128)S(1)} %copy.104, f32[8,12,64,128]{3,2,1,0:T(8,128)} %bitcast.154), kind=kOutput, calls=%fused_computation.47 | convolution fusion | flops 9437184 | bytes 3539328 | tf_op jit(solution)/shard_map/kh,khnp->hnp/dot_general | solution.py:23
  303.6 8.7 %fusion.14 = f32[1,256,4,12,128]{1,4,3,2,0:T(8,128)} fusion(f32[4,12,128,256]{3,2,1,0:T(8,128)} %fusion.9, f32[1,256,4,12,128]{1,4,3,2,0:T(8,128)} %copy.98, f32[12]{0:T(128)S(1)} %copy-done.26, f32[256,4,12]{0,2,1:T(8,128)S(1)} %copy-done.10, f32[4,12,64,128]{3,2,1,0:T(8,128)S(1)} %get-tuple-element.89, f32[12,64,128]{2,1,0:T(8,128)S(1)} %bitcast.155, ...), kind=kOutput, calls=%fused_computation.27 | convolution fusion | flops 1215037440 | bytes 21020912 | tf_op jit(solution)/shard_map/ncqt,cqhnp->qtchp/dot_general | solution.py:77
  312.3 8.1 %copy.99 = f32[256,4,1536]{2,1,0:T(4,128)} copy(f32[256,4,1536]{0,2,1:T(8,128)} %bitcast.151) | data formatting | bytes 12582912 | tf_op jit(solution)/shard_map/reshape | solution.py:83
  320.5 8.3 %multiply_reduce_fusion = (f32[256,4]{1,0:T(8,128)S(1)}, f32[256,4,1536]{2,1,0:T(4,128)}) fusion(f32[256,4,1536]{2,1,0:T(4,128)} %copy.99, bf16[256,4,1536]{2,1,0:T(4,128)(2,1)S(1)} %copy-done.5), kind=kLoop, calls=%fused_computation.32 | loop fusion | flops 12581888 | bytes 15732736 | tf_op jit(solution)/shard_map/reduce_sum | solution.py:86
  328.8 11.5 %psum.15 = f32[1,256,4]{2,1,0:T(8,128)S(1)} all-reduce(f32[1,256,4]{2,1,0:T(8,128)S(1)} %bitcast.157), channel_id=1, replica_groups=mesh['seq'=8,'head'=4] {'head'}, use_global_device_ids=true, to_apply=%region_9.10 | all-reduce | flops 1024 | bytes 8192 | tf_op jit(solution)/shard_map/psum | solution.py:86
  340.3 5.9 %multiply_convert_fusion.4 = bf16[256,4,1536]{2,1,0:T(4,128)(2,1)} fusion(f32[256,4,1536]{2,1,0:T(4,128)} %get-tuple-element.170, f32[1536]{0:T(1024)S(1)} %copy-done.21, f32[256,4]{1,0:T(8,128)S(1)} %rsqrt_bitcast_fusion), kind=kLoop, calls=%fused_computation.31 | loop fusion | flops 4718592 | bytes 9447424 | tf_op jit(solution)/shard_map/convert_element_type | solution.py:88
  (111 shorter events, 2.5 us)
Async XLA Ops:
  6.5 9.1 %copy-start.8 = (bf16[64,1024]{1,0:T(8,128)(2,1)S(1)}, bf16[64,1024]{1,0:T(8,128)(2,1)}, u32[]{:S(2)}) copy-start(bf16[64,1024]{1,0:T(8,128)(2,1)} %param.22) | copy-start | bytes 393220
  6.5 90.5 %all-gather.7.cloned.1.call-start = ((), (), s32[]{:S(2)}) async-start(), calls=%async_computation.1 | async-start | bytes 3538944 | tf_op jit(solution)/shard_map/all_gather | solution.py:26
  7.7 8.7 %copy-start.11 = (f32[256,12,4]{0,1,2:T(8,128)}, f32[256,12,4]{0,1,2:T(8,128)S(1)}, u32[]{:S(2)}) copy-start(f32[256,12,4]{0,1,2:T(8,128)S(1)} %fusion.54) | copy-start | bytes 147460
  20.8 9.9 %copy-start.2 = (bf16[32,32,1536]{2,1,0:T(8,128)(2,1)S(1)}, bf16[32,32,1536]{2,1,0:T(8,128)(2,1)}, u32[]{:S(2)}) copy-start(bf16[32,32,1536]{2,1,0:T(8,128)(2,1)} %param.19) | copy-start | bytes 9437188
  30.0 0.8 copy-start.1
  51.6 9.2 %copy-start.7 = (bf16[64,1024]{1,0:T(8,128)(2,1)S(1)}, bf16[64,1024]{1,0:T(8,128)(2,1)}, u32[]{:S(2)}) copy-start(bf16[64,1024]{1,0:T(8,128)(2,1)} %param.23) | copy-start | bytes 393220
  51.6 9.3 %copy-start.28 = (u32[32]{0:T(128)S(1)}, u32[32]{0:T(128)}, u32[]{:S(2)}) copy-start(u32[32]{0:T(128)} %constant.52) | copy-start | bytes 388
  51.6 35.4 %copy-start.9 = (bf16[64,1024]{1,0:T(8,128)(2,1)S(1)}, bf16[64,1024]{1,0:T(8,128)(2,1)}, u32[]{:S(2)}) copy-start(bf16[64,1024]{1,0:T(8,128)(2,1)} %param.22) | copy-start | bytes 393220
  51.6 36.0 %copy-start.12 = (f32[256,12,4]{0,1,2:T(8,128)S(1)}, f32[256,12,4]{0,1,2:T(8,128)}, u32[]{:S(2)}) copy-start(f32[256,12,4]{0,1,2:T(8,128)} %copy-done.11) | copy-start | bytes 147460
  51.6 36.0 %copy-start.16 = (f32[12,4,256]{2,0,1:T(8,128)S(1)}, f32[12,4,256]{2,0,1:T(8,128)}, u32[]{:S(2)}) copy-start(f32[12,4,256]{2,0,1:T(8,128)} %get-tuple-element.184) | copy-start | bytes 147460
  86.6 0.7 copy-start.24
  86.7 0.7 copy-start.22
  87.0 0.6 copy-start.18
  87.6 15.6 %copy-start.6 = (f32[4,12,64,128]{3,2,1,0:T(8,128)S(1)}, f32[4,12,64,128]{3,2,1,0:T(8,128)}, u32[]{:S(2)}) copy-start(f32[4,12,64,128]{3,2,1,0:T(8,128)} %get-tuple-element.85) | copy-start | bytes 4718596
  87.6 15.6 %copy-start.15 = (f32[4,256,12]{1,2,0:T(8,128)S(1)}, f32[4,256,12]{1,2,0:T(8,128)}, u32[]{:S(2)}) copy-start(f32[4,256,12]{1,2,0:T(8,128)} %get-tuple-element.182) | copy-start | bytes 147460
  87.6 15.7 %copy-start.27 = (f32[12]{0:T(128)S(1)}, f32[12]{0:T(128)}, u32[]{:S(2)}) copy-start(f32[12]{0:T(128)} %param.26) | copy-start | bytes 148
  124.6 14.8 %copy-start.4 = (bf16[32,32,1536]{2,1,0:T(8,128)(2,1)S(1)}, bf16[32,32,1536]{2,1,0:T(8,128)(2,1)}, u32[]{:S(2)}) copy-start(bf16[32,32,1536]{2,1,0:T(8,128)(2,1)} %param.20) | copy-start | bytes 9437188
  124.6 14.8 %copy-start.20 = (f32[1536]{0:T(1024)S(1)}, f32[1536]{0:T(1024)}, u32[]{:S(2)}) copy-start(f32[1536]{0:T(1024)} %param.27) | copy-start | bytes 18436
  147.3 74.6 %all-to-all-start = ((bf16[32,32,1536]{2,0,1:T(8,128)(2,1)}), bf16[32,32,1536]{2,0,1:T(8,128)(2,1)S(1)}, u32[]{:S(2)}, u32[]{:S(2)}) async-start(bf16[32,32,1536]{2,0,1:T(8,128)(2,1)} %copy.87), calls=%async_computation | async-start | bytes 6291456 | tf_op jit(solution)/shard_map/all_to_all | solution.py:126
  151.0 146.4 %all-gather.9.cloned.1.call-start = ((), (), s32[]{:S(2)}) async-start(), calls=%async_computation.2 | async-start | bytes 3538944 | tf_op jit(solution)/shard_map/all_gather | solution.py:26
  158.3 0.7 copy-start.13
  222.0 1.7 copy-start.3
  237.3 0.7 copy-start
  248.8 29.8 %copy-start.23 = (pred[8,8]{1,0:T(8,128)(4,1)S(1)}, pred[8,8]{1,0:T(8,128)(4,1)}, u32[]{:S(2)}) copy-start(pred[8,8]{1,0:T(8,128)(4,1)} %copy-done.22) | copy-start | bytes 196
  248.8 29.9 %copy-start.25 = (pred[8]{0:T(512)(128)(4,1)S(1)}, pred[8]{0:T(512)(128)(4,1)}, u32[]{:S(2)}) copy-start(pred[8]{0:T(512)(128)(4,1)} %copy-done.24) | copy-start | bytes 28
  248.8 30.0 %copy-start.14 = (f32[256,12,4]{0,1,2:T(8,128)S(1)}, f32[256,12,4]{0,1,2:T(8,128)}, u32[]{:S(2)}) copy-start(f32[256,12,4]{0,1,2:T(8,128)} %copy-done.13) | copy-start | bytes 147460
  248.8 30.0 %copy-start.17 = (f32[12,4,256]{2,0,1:T(8,128)S(1)}, f32[12,4,256]{2,0,1:T(8,128)}, u32[]{:S(2)}) copy-start(f32[12,4,256]{2,0,1:T(8,128)} %get-tuple-element.183) | copy-start | bytes 147460
  248.8 30.0 %copy-start.19 = (pred[256,256]{1,0:T(8,128)(4,1)S(1)}, pred[256,256]{1,0:T(8,128)(4,1)}, u32[]{:S(2)}) copy-start(pred[256,256]{1,0:T(8,128)(4,1)} %copy-done.18) | copy-start | bytes 196612
  278.9 24.7 %copy-start.10 = (f32[256,4,12]{0,2,1:T(8,128)S(1)}, f32[256,4,12]{0,2,1:T(8,128)}, u32[]{:S(2)}) copy-start(f32[256,4,12]{0,2,1:T(8,128)} %get-tuple-element.180) | copy-start | bytes 147460
  278.9 24.7 %copy-start.26 = (f32[12]{0:T(128)S(1)}, f32[12]{0:T(128)}, u32[]{:S(2)}) copy-start(f32[12]{0:T(128)} %param.32) | copy-start | bytes 148
  312.3 8.1 %copy-start.5 = (bf16[256,4,1536]{2,1,0:T(4,128)(2,1)S(1)}, bf16[256,4,1536]{2,1,0:T(4,128)(2,1)}, u32[]{:S(2)}) copy-start(bf16[256,4,1536]{2,1,0:T(4,128)(2,1)} %param.21) | copy-start | bytes 9437188
  320.5 19.8 %copy-start.21 = (f32[1536]{0:T(1024)S(1)}, f32[1536]{0:T(1024)}, u32[]{:S(2)}) copy-start(f32[1536]{0:T(1024)} %param.33) | copy-start | bytes 18436
Sparse Core Ops, SparseCore 0:
  30.9 63.2 all-gather.6
  238.2 59.1 all-gather.8
where the time goes:
time: 360 us; the launch traced here: 354 us
  local copies, waits for them, and re-layouts  105 us (29%)
  waiting for transfers between devices  70.9 us (20%)
  matrix products  62.3 us (17%)
  blocking collectives  61.8 us (17%)
  other arithmetic  35.1 us (10%)
  between operations  14.9 us (4%)
  starting transfers between devices  3.69 us (1%)
    all_to_all x1, waiting for transfers between devices, body(): lax.all_to_all(first_out.reshape(grid_rows, grid_cols, features), 'seq',...  61.5 us
    unnamed x2, blocking collectives  44.5 us
    convert_element_type x4, local copies, waits for them, and re-layouts, ssd_layer(): outputs = inner_part + from_state * lifting + skip_vec[:, None] * inputs  31.1 us
    dot_general x2, matrix products, ssd_layer(): jnp.einsum('ncqt,cqhnp->qtchp', read_mat.astype(jnp.float32), incoming, p...  20.7 us
    dot_general x2, matrix products, ssd_layer(): jnp.einsum('hcqts,qschp->qtchp', mixing, inputs, preferred_element_type=j...  18.6 us
    psum x2, blocking collectives, ssd_layer(): squares = lax.psum(jnp.sum(gated * gated, axis=-1), 'head')  17.3 us
    reshape x2, local copies, waits for them, and re-layouts, ssd_layer(): outputs.reshape(block_count, length, col_count, features)  17.1 us
    convert_element_type x2, local copies, waits for them, and re-layouts, ssd_layer(): gate_mat.astype(jnp.float32)  16.5 us
  transfers between devices with their start and end apart: 3, of which 2 were waited for; matrix products, arithmetic and copies ran while one was open for 23% of the time, Pallas kernels for 0%

commit v1 on v0

v1 whole, which is shorter than its diff:
```python
import functools
import jax
import jax.numpy as jnp
from jax import lax
from jax.experimental import pallas as pl
from jax.experimental.pallas import tpu as pltpu
from jax.sharding import PartitionSpec as P

BLOCK = 256
LANES = 128
EPSILON = 1e-05
LOG2E = 1.4426950408889634
HIGHEST = lax.Precision.HIGHEST
MESH = pl.DeviceIdType.MESH
F32 = jnp.float32
BF16 = jnp.bfloat16
VMEM_BYTES = 60 * 1024 * 1024


def contract(a, b, dims, precision=None):
    return lax.dot_general(
        a, b, (dims, ((), ())), precision=precision, preferred_element_type=F32
    )


def iota(shape, axis):
    return lax.broadcasted_iota(jnp.int32, shape, axis)


def block_sums(decay):
    upper = (iota((BLOCK, BLOCK), 0) <= iota((BLOCK, BLOCK), 1)).astype(F32)
    cumulative = contract(decay, upper, ((1,), (0,)), HIGHEST)
    total = contract(decay, jnp.ones((BLOCK, LANES), F32), ((1,), (0,)), HIGHEST)
    return cumulative, total


def head_state(write32, weight_row, tokens):
    loaded = (write32 * weight_row).astype(BF16)
    return contract(loaded, tokens, ((1,), (0,)))


def states_kernel(heads, x_ref, write_ref, step_ref, decay_ref, end_ref, total_ref):
    step_at = pl.program_id(0)

    @pl.when(step_at == 0)
    def _():
        end_ref[...] = jnp.zeros_like(end_ref)
        total_ref[...] = jnp.zeros_like(total_ref)

    cumulative, total = block_sums(decay_ref[...] * LOG2E)
    tokens = x_ref[...].reshape(BLOCK, x_ref.shape[-1])
    write32 = write_ref[...].astype(F32)
    final = total[:, :1]
    weights = jnp.exp2(final - cumulative) * step_ref[...]
    fade = jnp.exp2(total)
    for h in range(heads):
        gained = head_state(write32, weights[h : h + 1], tokens[:, h * LANES : (h + 1) * LANES])
        end_ref[h] = fade[h : h + 1] * end_ref[h] + gained
    total_ref[...] += total


def main_kernel(
    heads, skip_ref, x_ref, gate_ref, write_ref, read_ref, step_ref, decay_ref, prior_ref,
    gated_ref, squares_ref, state,
):
    @pl.when(pl.program_id(0) == 0)
    def _():
        state[...] = prior_ref[...].astype(F32)

    decay = decay_ref[...] * LOG2E
    step = step_ref[...]
    cumulative, total = block_sums(decay)
    lower = (iota((BLOCK, BLOCK), 0) >= iota((BLOCK, BLOCK), 1)).astype(F32)
    across = contract(lower, decay, ((1,), (1,)), HIGHEST)
    lifting = jnp.exp2(across)
    tokens = x_ref[...].reshape(BLOCK, x_ref.shape[-1])
    write = write_ref[...]
    read = read_ref[...]
    write32 = write.astype(F32)
    scores = contract(read, write, ((0,), (0,))) * lower
    weights = jnp.exp2(total[:, :1] - cumulative) * step
    fade = jnp.exp2(total)
    squares = jnp.zeros((BLOCK, LANES), F32)
    for h in range(heads):
        lanes = slice(h * LANES, (h + 1) * LANES)
        own = tokens[:, lanes]
        spread = jnp.minimum(across[:, h : h + 1] - cumulative[h : h + 1], 0.0)
        mixing = (jnp.exp2(spread) * scores * step[h : h + 1]).astype(BF16)
        held = state[h]
        out = contract(mixing, own, ((1,), (0,)))
        out += lifting[:, h : h + 1] * contract(read, held.astype(BF16), ((0,), (0,)))
        out += skip_ref[h] * own.astype(F32)
        gate = gate_ref[0, :, lanes].astype(F32)
        gated = out * (gate / (1.0 + jnp.exp2(gate * -LOG2E)))
        squares += gated * gated
        gated_ref[0, :, lanes] = gated.astype(BF16)
        state[h] = fade[h : h + 1] * held + head_state(write32, weights[h : h + 1], own)
    squares_ref[0] = contract(jnp.ones((8, LANES), F32), squares, ((1,), (1,)), HIGHEST)


def norm_kernel(inner, cols, gated_ref, squares_ref, gain_ref, out_ref):
    high = BLOCK // cols
    to = iota((BLOCK, BLOCK), 0)
    source = (to % high) * cols + to // high
    chosen = source == iota((BLOCK, BLOCK), 1)
    sums = contract(chosen.astype(F32), squares_ref[0], ((1,), (1,)), HIGHEST)
    scaled = lax.rsqrt(sums[:, :1] / inner + EPSILON)
    if cols > 1:
        gated = contract(chosen.astype(BF16), gated_ref[0], ((1,), (0,)))
    else:
        gated = gated_ref[0].astype(F32)
    result = gated * scaled * gain_ref[...]
    out_ref[...] = result.reshape(out_ref.shape).astype(BF16)


def greet(axis, count):
    me = lax.axis_index(axis)
    barrier = pltpu.get_barrier_semaphore()
    for hop in range(1, count):
        pl.semaphore_signal(
            barrier, inc=1, device_id={axis: lax.rem(me + hop, count)}, device_id_type=MESH
        )
    pl.semaphore_wait(barrier, count - 1)
    return me


def sum_kernel(count, own_ref, out_ref, held, send_sems, recv_sems):
    me = greet("head", count)
    copies = []
    for hop in range(1, count):
        copy = pltpu.make_async_remote_copy(
            src_ref=own_ref,
            dst_ref=held.at[hop - 1],
            send_sem=send_sems.at[hop - 1],
            recv_sem=recv_sems.at[hop - 1],
            device_id={"head": lax.rem(me + hop, count)},
            device_id_type=MESH,
        )
        copy.start()
        copies.append(copy)
    for copy in copies:
        copy.wait()
    total = own_ref[...]
    for hop in range(1, count):
        total += held[hop - 1]
    out_ref[...] = total


def trade_kernel(count, own_ref, out_ref, send_sems, recv_sems, local_sem):
    me = greet("seq", count)
    copies = []
    for hop in range(count // 2, count // 2 + count - 1):
        ahead = 1 + (hop - 1) % (count - 1)
        to = lax.rem(me + ahead, count)
        copy = pltpu.make_async_remote_copy(
            src_ref=own_ref.at[to],
            dst_ref=out_ref.at[me],
            send_sem=send_sems.at[ahead - 1],
            recv_sem=recv_sems.at[ahead - 1],
            device_id={"seq": to},
            device_id_type=MESH,
        )
        copy.start()
        copies.append(copy)
    local = pltpu.make_async_copy(own_ref.at[me], out_ref.at[me], local_sem)
    local.start()
    local.wait()
    for copy in copies:
        copy.wait()


def prior_kernel(
    count, end_ref, total_ref, prior_ref, totals, sent, swapped, pair, pairs, back, start, landed,
    total_send, total_recv, swap_sems, pair_send, pair_recv, back_sems,
):
    heads = end_ref.shape[0]
    half = heads // 2
    me = greet("seq", count)
    place = lax.rem(me, 2)
    partner = me + 1 - 2 * place
    group = me // 2
    groups = count // 2
    keep = place * half
    give = half - keep

    sent[...] = end_ref[pl.ds(give, half)].astype(BF16)
    swap = pltpu.make_async_remote_copy(
        src_ref=sent, dst_ref=swapped, send_sem=swap_sems.at[0], recv_sem=swap_sems.at[1],
        device_id={"seq": partner}, device_id_type=MESH,
    )
    swap.start()
    total_copies = []
    for hop in range(1, count):
        copy = pltpu.make_async_remote_copy(
            src_ref=total_ref, dst_ref=totals.at[hop], send_sem=total_send.at[hop - 1],
            recv_sem=total_recv.at[hop - 1],
            device_id={"seq": lax.rem(me + hop, count)}, device_id_type=MESH,
        )
        copy.start()
        total_copies.append(copy)
    totals[0] = total_ref[...]
    for copy in total_copies:
        copy.wait()
    swap.wait()

    def total_of(device):
        return totals[lax.rem(me - device + count, count)]

    odd = place.astype(F32)
    even_total = total_of(group * 2)
    odd_total = total_of(group * 2 + 1)
    odd_fade = jnp.exp2(odd_total)
    even_fade = jnp.exp2(even_total)
    for h in range(half):
        mine = end_ref[keep + h]
        other = swapped[h].astype(F32)
        first = odd * other + (1.0 - odd) * mine
        last = odd * mine + (1.0 - odd) * other
        row = jnp.where(place == 0, odd_fade[h : h + 1], odd_fade[half + h : half + h + 1])
        pair[h] = (row * first + last).astype(BF16)
        start[h] = first

    def pair_copy(hop):
        return pltpu.make_async_remote_copy(
            src_ref=pair, dst_ref=pairs.at[hop - 1], send_sem=pair_send.at[hop - 1],
            recv_sem=pair_recv.at[hop - 1],
            device_id={"seq": lax.rem(me + 2 * hop, count)}, device_id_type=MESH,
        )

    for hop in range(1, groups):

        @pl.when(group + hop < groups)
        def _():
            pair_copy(hop).start()

    for h in range(half):
        row = jnp.where(place == 0, even_fade[h : h + 1], even_fade[half + h : half + h + 1])
        back[h] = jnp.broadcast_to(row, back.shape[1:])

    span = jnp.zeros(total_ref.shape, F32)
    prior_ref[pl.ds(keep, half)] = jnp.zeros((half,) + prior_ref.shape[1:], F32)
    for hop in range(1, groups):

        @pl.when(group >= hop)
        def _():
            pair_copy(hop).wait_recv()
            factor = jnp.exp2(span)
            for h in range(half):
                row = jnp.where(place == 0, factor[h : h + 1], factor[half + h : half + h + 1])
                prior_ref[keep + h] += row * pairs[hop - 1, h].astype(F32)

        source = lax.rem(group - hop + groups, groups) * 2
        span += total_of(source) + total_of(source + 1)

    for hop in range(1, groups):

        @pl.when(group + hop < groups)
        def _():
            pair_copy(hop).wait_send()

    for h in range(half):
        before = prior_ref[keep + h]
        later = back[h] * before + start[h]
        sent[h] = (odd * before + (1.0 - odd) * later).astype(BF16)
        prior_ref[keep + h] = odd * later + (1.0 - odd) * before
    answer = pltpu.make_async_remote_copy(
        src_ref=sent, dst_ref=landed, send_sem=back_sems.at[0], recv_sem=back_sems.at[1],
        device_id={"seq": partner}, device_id_type=MESH,
    )
    answer.start()
    answer.wait()
    prior_ref[pl.ds(give, half)] = landed[...].astype(F32)


def comm_params(number):
    return pltpu.CompilerParams(
        collective_id=number, has_side_effects=True, vmem_limit_bytes=VMEM_BYTES
    )


def carried_state(seq, end_state, totals, number):
    heads, size, width = end_state.shape
    half = heads // 2
    groups = seq // 2
    dma = pltpu.SemaphoreType.DMA
    whole = pl.BlockSpec(memory_space=pltpu.VMEM)
    return pl.pallas_call(
        functools.partial(prior_kernel, seq),
        out_shape=jax.ShapeDtypeStruct(end_state.shape, F32),
        in_specs=[whole, whole],
        out_specs=whole,
        scratch_shapes=[
            pltpu.VMEM((seq,) + totals.shape, F32),
            pltpu.VMEM((half, size, width), BF16),
            pltpu.VMEM((half, size, width), BF16),
            pltpu.VMEM((half, size, width), BF16),
            pltpu.VMEM((max(groups - 1, 1), half, size, width), BF16),
            pltpu.VMEM((half, size, width), F32),
            pltpu.VMEM((half, size, width), F32),
            pltpu.VMEM((half, size, width), BF16),
            dma((seq - 1,)),
            dma((seq - 1,)),
            dma((2,)),
            dma((max(groups - 1, 1),)),
            dma((max(groups - 1, 1),)),
            dma((2,)),
        ],
        compiler_params=comm_params(number),
        name=f"prior_{number}",
    )(end_state, totals)


def layer(seq, head, number, inputs, x_spec, gate, write_mat, read_mat, step_mat, decay_mat, skip):
    heads = step_mat.shape[0]
    size = write_mat.shape[0]
    blocks = step_mat.shape[1] // BLOCK
    features = gate.shape[-1]
    width = features // heads
    wide = pl.BlockSpec((size, BLOCK), lambda b: (0, b))
    thin = pl.BlockSpec((heads, BLOCK), lambda b: (0, b))
    rows = pl.BlockSpec((1, BLOCK, features), lambda b: (b, 0, 0))
    end_state, totals = pl.pallas_call(
        functools.partial(states_kernel, heads),
        grid=(blocks,),
        out_shape=(
            jax.ShapeDtypeStruct((heads, size, width), F32),
            jax.ShapeDtypeStruct((heads, LANES), F32),
        ),
        in_specs=[x_spec, wide, thin, thin],
        out_specs=(
            pl.BlockSpec((heads, size, width), lambda b: (0, 0, 0)),
            pl.BlockSpec((heads, LANES), lambda b: (0, 0)),
        ),
        name=f"states_{number}",
    )(inputs, write_mat, step_mat, decay_mat)
    prior = carried_state(seq, end_state, totals, number)
    gated, squares = pl.pallas_call(
        functools.partial(main_kernel, heads),
        grid=(blocks,),
        out_shape=(
            jax.ShapeDtypeStruct((blocks, BLOCK, features), BF16),
            jax.ShapeDtypeStruct((blocks, 8, BLOCK), F32),
        ),
        in_specs=[
            pl.BlockSpec(memory_space=pltpu.SMEM),
            x_spec,
            rows,
            wide,
            wide,
            thin,
            thin,
            pl.BlockSpec((heads, size, width), lambda b: (0, 0, 0)),
        ],
        out_specs=(rows, pl.BlockSpec((1, 8, BLOCK), lambda b: (b, 0, 0))),
        scratch_shapes=[pltpu.VMEM((heads, size, width), F32)],
        compiler_params=pltpu.CompilerParams(vmem_limit_bytes=VMEM_BYTES),
        name=f"main_{number}",
    )(skip, inputs, gate, write_mat, read_mat, step_mat, decay_mat, prior)
    whole = pl.BlockSpec(memory_space=pltpu.VMEM)
    squares = pl.pallas_call(
        functools.partial(sum_kernel, head),
        out_shape=jax.ShapeDtypeStruct(squares.shape, F32),
        in_specs=[whole],
        out_specs=whole,
        scratch_shapes=[
            pltpu.VMEM((head - 1,) + squares.shape, F32),
            pltpu.SemaphoreType.DMA((head - 1,)),
            pltpu.SemaphoreType.DMA((head - 1,)),
        ],
        compiler_params=comm_params(number + 2),
        name=f"squares_{number}",
    )(squares)
    return gated, squares


def normalise(head, gated, squares, gain, cols, out_shape, out_spec, number):
    features = gated.shape[-1]
    return pl.pallas_call(
        functools.partial(norm_kernel, features * head, cols),
        grid=(gated.shape[0],),
        out_shape=jax.ShapeDtypeStruct(out_shape, BF16),
        in_specs=[
            pl.BlockSpec((1, BLOCK, features), lambda b: (b, 0, 0)),
            pl.BlockSpec((1, 8, BLOCK), lambda b: (b, 0, 0)),
            pl.BlockSpec((1, features), lambda b: (0, 0)),
        ],
        out_specs=out_spec,
        compiler_params=pltpu.CompilerParams(vmem_limit_bytes=VMEM_BYTES),
        name=f"norm_{number}",
    )(gated, squares, gain.reshape(1, features))


def body(
    seq, head, tokens_in, gate_rows, gate_cols, write_rows, read_rows, step_rows, decay_rows,
    skip_rows, norm_rows, write_cols, read_cols, step_cols, decay_cols, skip_cols, norm_cols,
):
    grid_rows, grid_cols, features = tokens_in.shape
    blocks = grid_rows * grid_cols // BLOCK
    high = BLOCK // grid_cols
    local_cols = grid_cols // seq
    all_rows = grid_rows * seq
    per_col = all_rows // BLOCK
    slabs = BLOCK // grid_rows

    first = layer(
        seq, head, 0, tokens_in.reshape(blocks, BLOCK, features),
        pl.BlockSpec((1, BLOCK, features), lambda b: (b, 0, 0)),
        gate_rows.reshape(blocks, BLOCK, features),
        write_rows, read_rows, step_rows, decay_rows, skip_rows,
    )
    hidden = normalise(
        head, *first, norm_rows, grid_cols, (seq, local_cols, grid_rows, features),
        pl.BlockSpec((seq, local_cols, high, features), lambda b: (0, 0, b, 0)), 0,
    )
    anywhere = pl.BlockSpec(memory_space=pl.ANY)
    dma = pltpu.SemaphoreType.DMA
    hidden = pl.pallas_call(
        functools.partial(trade_kernel, seq),
        out_shape=jax.ShapeDtypeStruct(hidden.shape, BF16),
        in_specs=[anywhere],
        out_specs=anywhere,
        scratch_shapes=[dma((seq - 1,)), dma((seq - 1,)), dma(())],
        compiler_params=comm_params(4),
        name="trade",
    )(hidden)
    gate = jnp.transpose(gate_cols, (1, 0, 2)).reshape(local_cols * per_col, BLOCK, features)
    second = layer(
        seq, head, 1, hidden,
        pl.BlockSpec(
            (slabs, 1, grid_rows, features), lambda b: (b % per_col, b // per_col, 0, 0)
        ),
        gate, write_cols, read_cols, step_cols, decay_cols, skip_cols,
    )
    result = normalise(
        head, *second, norm_cols, 1, (local_cols * per_col, BLOCK, features),
        pl.BlockSpec((1, BLOCK, features), lambda b: (b, 0, 0)), 1,
    )
    return jnp.transpose(result.reshape(local_cols, all_rows, features), (1, 0, 2))


def solution(mesh):
    placed = (
        P("seq", None, "head"),
        P("seq", None, "head"),
        P(None, "seq", "head"),
        P(None, "seq"),
        P(None, "seq"),
        P("head", "seq"),
        P("head", "seq"),
        P("head"),
        P("head"),
        P(None, "seq"),
        P(None, "seq"),
        P("head", "seq"),
        P("head", "seq"),
        P("head"),
        P("head"),
    )
    return jax.shard_map(
        functools.partial(body, mesh.shape["seq"], mesh.shape["head"]),
        mesh=mesh, in_specs=placed, out_specs=P(None, "seq", "head"), check_vma=False,
    )
```

time: 360 us -> 183 us (0.51); the launches traced: 354 us -> 181 us
  Pallas kernels: 0 us -> 172 us
  local copies, waits for them, and re-layouts: 105 us -> 9.43 us
  waiting for transfers between devices: 70.9 us -> 0 us
  matrix products: 62.3 us -> 0 us
  blocking collectives: 61.8 us -> 0 us
  other arithmetic: 35.1 us -> 0 us
  between operations: 14.9 us -> 0.09 us
  starting transfers between devices: 3.69 us -> 0 us
    pallas_call x0 -> x11, Pallas kernels: none -> 172 us  [the longest x1 75.5 us: body(): pl.pallas_call(functools.partial(trade_kernel, seq), out_shape=jax.ShapeD...]
    dot_general x12 -> x0, matrix products: 62.3 us -> none  [the longest x2 20.7 us: ssd_layer(): jnp.einsum('ncqt,cqhnp->qtchp', read_mat.astype(jnp.float32), incoming, p...]
    all_to_all x1 -> x0, waiting for transfers between devices: 61.5 us -> none  [body(): lax.all_to_all(first_out.reshape(grid_rows, grid_cols, features), 'seq',...]
    convert_element_type x9 -> x0, local copies, waits for them, and re-layouts: 52.7 us -> none  [the longest x4 31.1 us: ssd_layer(): outputs = inner_part + from_state * lifting + skip_vec[:, None] * inputs]
    unnamed x2 -> x0, blocking collectives: 44.5 us -> none
    psum x2 -> x0, blocking collectives: 17.3 us -> none  [ssd_layer(): squares = lax.psum(jnp.sum(gated * gated, axis=-1), 'head')]
    reshape x3 -> x2, local copies, waits for them, and re-layouts: 18 us -> 1.2 us  [normalise(): gain.reshape(1, features)]
    another operation x11 -> x0, local copies, waits for them, and re-layouts: 16.3 us -> none
  transfers between devices with their start and end apart: 3 -> 0, of which waited for: 2 -> 0; matrix products, arithmetic and copies ran while one was open for 23% -> 0% of each run, Pallas kernels for 0% -> 0%
where the time goes in v1:
time: 183 us; the launch traced here: 181 us
  Pallas kernels  172 us (94%)
  local copies, waits for them, and re-layouts  9.43 us (5%)
    pallas_call x1, Pallas kernels, body(): pl.pallas_call(functools.partial(trade_kernel, seq), out_shape=jax.ShapeD...  75.5 us
    pallas_call x2, Pallas kernels, carried_state(): pl.pallas_call(functools.partial(prior_kernel, seq), out_shape=jax.ShapeD...  39.1 us
    pallas_call x2, Pallas kernels, layer(): pl.pallas_call(functools.partial(main_kernel, heads), grid=(blocks,), out...  25 us
    pallas_call x2, Pallas kernels, layer(): pl.pallas_call(functools.partial(sum_kernel, head), out_shape=jax.ShapeDt...  11 us
    pallas_call x2, Pallas kernels, normalise(): pl.pallas_call(functools.partial(norm_kernel, features * head, cols), gri...  11 us
    pallas_call x2, Pallas kernels, layer(): pl.pallas_call(functools.partial(states_kernel, heads), grid=(blocks,), o...  10.3 us
    transpose x1, local copies, waits for them, and re-layouts, body(): jnp.transpose(result.reshape(local_cols, all_rows, features), (1, 0, 2))  5.98 us

profile of v1, /device:TPU:0, one launch (start us, length us, event | category | flops | bytes accessed | tf_op | source)
XLA Modules:
  0.0 181.5 jit_solution(9593615650832395693)
XLA Ops:
  0.0 5.1 %states_0.1 = (f32[12,64,128]{2,1,0:T(8,128)}, f32[12,128]{1,0:T(8,128)}) custom-call(bf16[4,256,1536]{2,1,0:T(8,128)(2,1)} %bitcast.7, bf16[64,1024]{1,0:T(8,128)(2,1)} %write_ref.5, f32[12,1024]{1,0:T(8,128)} %step_ref.5, f32[12,1024]{1,0:T(8,128)} %decay_ref.5), custom_call_target="tpu_custom_call" | custom-call | tf_op jit(solution)/shard_map/states_0/pallas_call | solution.py:322
  5.1 21.7 %prior_0.1.prior_ref = f32[12,64,128]{2,1,0:T(8,128)} custom-call(f32[12,64,128]{2,1,0:T(8,128)} %get-tuple-element.13.end_ref, f32[12,128]{1,0:T(8,128)} %get-tuple-element.14.total_ref), custom_call_target="tpu_custom_call" | custom-call | tf_op jit(solution)/shard_map/prior_0/pallas_call | solution.py:287
  26.8 0.0 copy-start.1
  26.8 12.8 %main_0.1 = (bf16[4,256,1536]{2,1,0:T(8,128)(2,1)}, f32[4,8,256]{2,1,0:T(8,128)}) custom-call(f32[12]{0:T(128)} %skip_ref.2, bf16[4,256,1536]{2,1,0:T(8,128)(2,1)} %bitcast.8, bf16[4,256,1536]{2,1,0:T(8,128)(2,1)} %bitcast.10, bf16[64,1024]{1,0:T(8,128)(2,1)} %write_ref.5, bf16[64,1024]{1,0:T(8,128)(2,1)} %read_ref.2, f32[12,1024]{1,0:T(8,128)} %step_ref.5, ...), custom_call_target="tpu_custom_call" | custom-call | tf_op jit(solution)/shard_map/main_0/pallas_call | solution.py:337
  39.6 5.5 %squares_0.1.squares_ref = f32[4,8,256]{2,1,0:T(8,128)} custom-call(f32[4,8,256]{2,1,0:T(8,128)} %get-tuple-element.16.own_ref), custom_call_target="tpu_custom_call" | custom-call | tf_op jit(solution)/shard_map/squares_0/pallas_call | solution.py:360
  45.1 0.0 copy-done.1
  45.1 0.6 reshape.14.gain_ref
  45.7 5.8 %norm_0.1.own_ref = bf16[8,4,32,1536]{3,2,1,0:T(8,128)(2,1)} custom-call(bf16[4,256,1536]{2,1,0:T(8,128)(2,1)} %get-tuple-element.15.gated_ref, f32[4,8,256]{2,1,0:T(8,128)} %squares_0.1.squares_ref, f32[1,1536]{1,0:T(1,128)} %reshape.14.gain_ref), custom_call_target="tpu_custom_call" | custom-call | tf_op jit(solution)/shard_map/norm_0/pallas_call | solution.py:378
  51.4 75.5 %trade.1.x_ref = bf16[8,4,32,1536]{3,2,1,0:T(8,128)(2,1)} custom-call(bf16[8,4,32,1536]{3,2,1,0:T(8,128)(2,1)} %norm_0.1.own_ref), custom_call_target="tpu_custom_call" | custom-call | tf_op jit(solution)/shard_map/trade/pallas_call | solution.py:417
  127.0 0.0 copy-start
  127.0 5.2 %states_1.1 = (f32[12,64,128]{2,1,0:T(8,128)}, f32[12,128]{1,0:T(8,128)}) custom-call(bf16[8,4,32,1536]{3,2,1,0:T(8,128)(2,1)} %trade.1.x_ref, bf16[64,1024]{1,0:T(8,128)(2,1)} %write_ref.7, f32[12,1024]{1,0:T(8,128)} %step_ref.7, f32[12,1024]{1,0:T(8,128)} %decay_ref.7), custom_call_target="tpu_custom_call" | custom-call | tf_op jit(solution)/shard_map/states_1/pallas_call | solution.py:322
  132.2 17.4 %prior_1.1.prior_ref = f32[12,64,128]{2,1,0:T(8,128)} custom-call(f32[12,64,128]{2,1,0:T(8,128)} %get-tuple-element.17.end_ref, f32[12,128]{1,0:T(8,128)} %get-tuple-element.18.total_ref), custom_call_target="tpu_custom_call" | custom-call | tf_op jit(solution)/shard_map/prior_1/pallas_call | solution.py:287
  149.7 0.0 copy-done
  149.7 2.2 %copy.19 = bf16[256,4,1536]{2,0,1:T(8,128)(2,1)} copy(bf16[256,4,1536]{2,1,0:T(4,128)(2,1)S(1)} %copy-done) | data formatting | bytes 6291456 | tf_op args[2]
  151.9 0.0 copy-start.2
  151.9 12.3 %main_1.1 = (bf16[4,256,1536]{2,1,0:T(8,128)(2,1)}, f32[4,8,256]{2,1,0:T(8,128)}) custom-call(f32[12]{0:T(128)} %skip_ref.3, bf16[8,4,32,1536]{3,2,1,0:T(8,128)(2,1)} %trade.1.x_ref, bf16[4,256,1536]{2,1,0:T(8,128)(2,1)} %bitcast.6, bf16[64,1024]{1,0:T(8,128)(2,1)} %write_ref.7, bf16[64,1024]{1,0:T(8,128)(2,1)} %read_ref.3, f32[12,1024]{1,0:T(8,128)} %step_ref.7, ...), custom_call_target="tpu_custom_call" | custom-call | tf_op jit(solution)/shard_map/main_1/pallas_call | solution.py:337
  164.2 5.5 %squares_1.1.squares_ref = f32[4,8,256]{2,1,0:T(8,128)} custom-call(f32[4,8,256]{2,1,0:T(8,128)} %get-tuple-element.20.own_ref), custom_call_target="tpu_custom_call" | custom-call | tf_op jit(solution)/shard_map/squares_1/pallas_call | solution.py:360
  169.7 0.0 copy-done.2
  169.7 0.6 reshape.15.gain_ref
  170.3 5.2 %norm_1.1 = bf16[4,256,1536]{2,1,0:T(8,128)(2,1)} custom-call(bf16[4,256,1536]{2,1,0:T(8,128)(2,1)} %get-tuple-element.19.gated_ref, f32[4,8,256]{2,1,0:T(8,128)} %squares_1.1.squares_ref, f32[1,1536]{1,0:T(1,128)} %reshape.15.gain_ref), custom_call_target="tpu_custom_call" | custom-call | tf_op jit(solution)/shard_map/norm_1/pallas_call | solution.py:378
  175.5 6.0 %copy.17 = bf16[256,4,1536]{2,1,0:T(4,128)(2,1)} copy(bf16[256,4,1536]{2,0,1:T(8,128)(2,1)} %bitcast.9) | data formatting | bytes 6291456 | tf_op jit(solution)/shard_map/transpose | solution.py:438
Async XLA Ops:
  26.8 18.3 %copy-start.1 = (f32[1536]{0:T(1024)S(1)}, f32[1536]{0:T(1024)}, u32[]{:S(2)}) copy-start(f32[1536]{0:T(1024)} %param.23) | copy-start | bytes 18436
  127.0 22.7 %copy-start = (bf16[256,4,1536]{2,1,0:T(4,128)(2,1)S(1)}, bf16[256,4,1536]{2,1,0:T(4,128)(2,1)}, u32[]{:S(2)}) copy-start(bf16[256,4,1536]{2,1,0:T(4,128)(2,1)} %param.17) | copy-start | bytes 9437188
  151.9 17.8 %copy-start.2 = (f32[1536]{0:T(1024)S(1)}, f32[1536]{0:T(1024)}, u32[]{:S(2)}) copy-start(f32[1536]{0:T(1024)} %param.29) | copy-start | bytes 18436

commit v2 on v1

--- a/solution.py
+++ b/solution.py
@@ -39,7 +39,24 @@
     return contract(loaded, tokens, ((1,), (0,)))
 
 
-def states_kernel(heads, x_ref, write_ref, step_ref, decay_ref, end_ref, total_ref):
+def column_scale(local_cols, per_col, grid_rows, grid_cols, place_ref, scales):
+    high = BLOCK // grid_cols
+    column = place_ref[0] * local_cols + pl.program_id(0) // per_col
+    shape = (BLOCK, scales.shape[0])
+    row = iota(shape, 0)
+    depth = scales.shape[0] * grid_rows // BLOCK
+    source = (row // grid_rows) * depth + (row % grid_rows) // high
+    picked = contract((iota(shape, 1) == source).astype(F32), scales, ((1,), (0,)), HIGHEST)
+    lane = (iota((BLOCK, BLOCK), 0) % high) * grid_cols + column
+    return jnp.sum(jnp.where(iota((BLOCK, BLOCK), 1) == lane, picked, 0.0), axis=1, keepdims=True)
+
+
+def states_kernel(heads, scale_of, *refs):
+    if scale_of is None:
+        x_ref, write_ref, step_ref, decay_ref, end_ref, total_ref = refs
+    else:
+        (place_ref, scales_ref, gain_ref, x_ref, write_ref, step_ref, decay_ref, end_ref,
+         total_ref, hidden_ref) = refs
     step_at = pl.program_id(0)
 
     @pl.when(step_at == 0)
@@ -49,23 +66,31 @@
 
     cumulative, total = block_sums(decay_ref[...] * LOG2E)
     tokens = x_ref[...].reshape(BLOCK, x_ref.shape[-1])
+    if scale_of is not None:
+        scale = scale_of(place_ref, scales_ref[...])
     write32 = write_ref[...].astype(F32)
     final = total[:, :1]
     weights = jnp.exp2(final - cumulative) * step_ref[...]
     fade = jnp.exp2(total)
     for h in range(heads):
-        gained = head_state(write32, weights[h : h + 1], tokens[:, h * LANES : (h + 1) * LANES])
+        lanes = slice(h * LANES, (h + 1) * LANES)
+        own = tokens[:, lanes]
+        if scale_of is not None:
+            own = (own.astype(F32) * scale * gain_ref[:, lanes]).astype(BF16)
+            hidden_ref[0, :, lanes] = own
+        gained = head_state(write32, weights[h : h + 1], own)
         end_ref[h] = fade[h : h + 1] * end_ref[h] + gained
     total_ref[...] += total
 
 
 def main_kernel(
-    heads, skip_ref, x_ref, gate_ref, write_ref, read_ref, step_ref, decay_ref, prior_ref,
+    heads, cols, skip_ref, x_ref, gate_ref, write_ref, read_ref, step_ref, decay_ref, prior_ref,
     gated_ref, squares_ref, state,
 ):
     @pl.when(pl.program_id(0) == 0)
     def _():
-        state[...] = prior_ref[...].astype(F32)
+        state[...] = prior_ref[...]
+        squares_ref[...] = jnp.zeros_like(squares_ref)
 
     decay = decay_ref[...] * LOG2E
     step = step_ref[...]
@@ -81,6 +106,10 @@
     weights = jnp.exp2(total[:, :1] - cumulative) * step
     fade = jnp.exp2(total)
     squares = jnp.zeros((BLOCK, LANES), F32)
+    read_twice = jnp.concatenate([read, read], axis=0)
+    high = BLOCK // cols
+    to = iota((BLOCK, BLOCK), 0)
+    chosen = ((to % high) * cols + to // high == iota((BLOCK, BLOCK), 1)).astype(BF16)
     for h in range(heads):
         lanes = slice(h * LANES, (h + 1) * LANES)
         own = tokens[:, lanes]
@@ -88,44 +117,58 @@
         mixing = (jnp.exp2(spread) * scores * step[h : h + 1]).astype(BF16)
         held = state[h]
         out = contract(mixing, own, ((1,), (0,)))
-        out += lifting[:, h : h + 1] * contract(read, held.astype(BF16), ((0,), (0,)))
+        coarse = held.astype(BF16)
+        fine = (held - coarse.astype(F32)).astype(BF16)
+        parts = jnp.concatenate([coarse, fine], axis=0)
+        out += lifting[:, h : h + 1] * contract(read_twice, parts, ((0,), (0,)))
         out += skip_ref[h] * own.astype(F32)
         gate = gate_ref[0, :, lanes].astype(F32)
         gated = out * (gate / (1.0 + jnp.exp2(gate * -LOG2E)))
         squares += gated * gated
-        gated_ref[0, :, lanes] = gated.astype(BF16)
+        if cols > 1:
+            moved = contract(chosen, gated.astype(BF16), ((1,), (0,)))
+            gated_ref[:, :, :, lanes] = moved.reshape(gated_ref.shape[:3] + (LANES,)).astype(BF16)
+        else:
+            gated_ref[0, :, lanes] = gated
         state[h] = fade[h : h + 1] * held + head_state(write32, weights[h : h + 1], own)
-    squares_ref[0] = contract(jnp.ones((8, LANES), F32), squares, ((1,), (1,)), HIGHEST)
-
-
-def norm_kernel(inner, cols, gated_ref, squares_ref, gain_ref, out_ref):
-    high = BLOCK // cols
-    to = iota((BLOCK, BLOCK), 0)
-    source = (to % high) * cols + to // high
-    chosen = source == iota((BLOCK, BLOCK), 1)
-    sums = contract(chosen.astype(F32), squares_ref[0], ((1,), (1,)), HIGHEST)
-    scaled = lax.rsqrt(sums[:, :1] / inner + EPSILON)
-    if cols > 1:
-        gated = contract(chosen.astype(BF16), gated_ref[0], ((1,), (0,)))
-    else:
-        gated = gated_ref[0].astype(F32)
-    result = gated * scaled * gain_ref[...]
-    out_ref[...] = result.reshape(out_ref.shape).astype(BF16)
-
-
-def greet(axis, count):
-    me = lax.axis_index(axis)
+    row = contract(jnp.ones((8, LANES), F32), squares, ((1,), (1,)), HIGHEST)
+    squares_ref[pl.ds(pl.program_id(0), 1), :] = row[:1]
+
+
+def norm_kernel(inner, per_col, gated_ref, squares_ref, gain_ref, out_ref):
+    cols, rows, features = gated_ref.shape
+    square = (BLOCK, BLOCK)
+    start = pl.program_id(0) * rows
+    lane = start % BLOCK + iota(square, 0) % rows
+    sums = contract((lane == iota(square, 1)).astype(F32), squares_ref[...], ((1,), (1,)), HIGHEST)
+    block = (iota(sums.shape, 0) // rows) * per_col + start // BLOCK
+    sums = jnp.sum(jnp.where(iota(sums.shape, 1) == block, sums, 0.0), axis=1, keepdims=True)
+    scaled = lax.rsqrt(sums / inner + EPSILON)
+    chosen = ((iota(square, 0) % cols) * rows + iota(square, 0) // cols == iota(square, 1)).astype(BF16)
+    for at in range(0, features, LANES):
+        lanes = slice(at, at + LANES)
+        result = gated_ref[:, :, lanes].reshape(BLOCK, LANES) * scaled * gain_ref[:, lanes]
+        result = result.astype(BF16)
+        if cols > 1:
+            moved = contract(chosen, result, ((1,), (0,)))
+            out_ref[:, :, lanes] = moved.reshape(rows, cols, LANES).astype(BF16)
+        else:
+            out_ref[:, lanes] = result
+
+
+def greet(axes):
     barrier = pltpu.get_barrier_semaphore()
-    for hop in range(1, count):
-        pl.semaphore_signal(
-            barrier, inc=1, device_id={axis: lax.rem(me + hop, count)}, device_id_type=MESH
-        )
-    pl.semaphore_wait(barrier, count - 1)
-    return me
-
-
-def sum_kernel(count, own_ref, out_ref, held, send_sems, recv_sems):
-    me = greet("head", count)
+    for axis, count in axes:
+        me = lax.axis_index(axis)
+        for hop in range(1, count):
+            pl.semaphore_signal(
+                barrier, inc=1, device_id={axis: lax.rem(me + hop, count)}, device_id_type=MESH
+            )
+    pl.semaphore_wait(barrier, sum(count - 1 for _, count in axes))
+
+
+def head_sum(count, own_ref, held, send_sems, recv_sems):
+    me = lax.axis_index("head")
     copies = []
     for hop in range(1, count):
         copy = pltpu.make_async_remote_copy(
@@ -143,11 +186,20 @@
     total = own_ref[...]
     for hop in range(1, count):
         total += held[hop - 1]
-    out_ref[...] = total
-
-
-def trade_kernel(count, own_ref, out_ref, send_sems, recv_sems, local_sem):
-    me = greet("seq", count)
+    return total
+
+
+def sum_kernel(count, own_ref, out_ref, held, send_sems, recv_sems):
+    greet((("head", count),))
+    out_ref[...] = head_sum(count, own_ref, held, send_sems, recv_sems)
+
+
+def trade_kernel(
+    count, heads, inner, own_ref, squares_ref, out_ref, scales_ref, held, scale, sum_send,
+    sum_recv, scale_send, scale_recv, send_sems, recv_sems, local_sem,
+):
+    greet((("seq", count), ("head", heads)))
+    me = lax.axis_index("seq")
     copies = []
     for hop in range(count // 2, count // 2 + count - 1):
         ahead = 1 + (hop - 1) % (count - 1)
@@ -164,18 +216,35 @@
         copies.append(copy)
     local = pltpu.make_async_copy(own_ref.at[me], out_ref.at[me], local_sem)
     local.start()
+    total = head_sum(heads, squares_ref, held, sum_send, sum_recv)
+    scale[...] = lax.rsqrt(total / inner + EPSILON)
+    depth = scale.shape[0]
+    mine = pl.ds(pl.multiple_of(me * depth, depth), depth)
+    for hop in range(1, count):
+        copy = pltpu.make_async_remote_copy(
+            src_ref=scale,
+            dst_ref=scales_ref.at[mine],
+            send_sem=scale_send.at[hop - 1],
+            recv_sem=scale_recv.at[hop - 1],
+            device_id={"seq": lax.rem(me + hop, count)},
+            device_id_type=MESH,
+        )
+        copy.start()
+        copies.append(copy)
+    scales_ref[mine, :] = scale[...]
     local.wait()
     for copy in copies:
         copy.wait()
 
 
 def prior_kernel(
-    count, end_ref, total_ref, prior_ref, totals, sent, swapped, pair, pairs, back, start, landed,
-    total_send, total_recv, swap_sems, pair_send, pair_recv, back_sems,
+    count, end_ref, total_ref, prior_ref, totals, sent, swapped, pair, pairs, back, start, landed, near,
+    near_sems, total_send, total_recv, swap_sems, pair_send, pair_recv, back_sems,
 ):
     heads = end_ref.shape[0]
     half = heads // 2
-    me = greet("seq", count)
+    greet((("seq", count),))
+    me = lax.axis_index("seq")
     place = lax.rem(me, 2)
     partner = me + 1 - 2 * place
     group = me // 2
@@ -189,6 +258,11 @@
         device_id={"seq": partner}, device_id_type=MESH,
     )
     swap.start()
+    near_copy = pltpu.make_async_remote_copy(
+        src_ref=total_ref, dst_ref=near, send_sem=near_sems.at[0], recv_sem=near_sems.at[1],
+        device_id={"seq": partner}, device_id_type=MESH,
+    )
+    near_copy.start()
     total_copies = []
     for hop in range(1, count):
         copy = pltpu.make_async_remote_copy(
@@ -199,18 +273,15 @@
         copy.start()
         total_copies.append(copy)
     totals[0] = total_ref[...]
-    for copy in total_copies:
-        copy.wait()
+    near_copy.wait()
     swap.wait()
 
     def total_of(device):
         return totals[lax.rem(me - device + count, count)]
 
     odd = place.astype(F32)
-    even_total = total_of(group * 2)
-    odd_total = total_of(group * 2 + 1)
-    odd_fade = jnp.exp2(odd_total)
-    even_fade = jnp.exp2(even_total)
+    odd_fade = jnp.exp2(jnp.where(place == 0, near[...], total_ref[...]))
+    even_fade = jnp.exp2(jnp.where(place == 0, total_ref[...], near[...]))
     for h in range(half):
         mine = end_ref[keep + h]
         other = swapped[h].astype(F32)
@@ -237,6 +308,8 @@
         row = jnp.where(place == 0, even_fade[h : h + 1], even_fade[half + h : half + h + 1])
         back[h] = jnp.broadcast_to(row, back.shape[1:])
 
+    for copy in total_copies:
+        copy.wait()
     span = jnp.zeros(total_ref.shape, F32)
     prior_ref[pl.ds(keep, half)] = jnp.zeros((half,) + prior_ref.shape[1:], F32)
     for hop in range(1, groups):
@@ -298,6 +371,8 @@
             pltpu.VMEM((half, size, width), F32),
             pltpu.VMEM((half, size, width), F32),
             pltpu.VMEM((half, size, width), BF16),
+            pltpu.VMEM(totals.shape, F32),
+            dma((2,)),
             dma((seq - 1,)),
             dma((seq - 1,)),
             dma((2,)),
@@ -310,7 +385,10 @@
     )(end_state, totals)
 
 
-def layer(seq, head, number, inputs, x_spec, gate, write_mat, read_mat, step_mat, decay_mat, skip):
+def layer(
+    seq, number, inputs, x_spec, gate, write_mat, read_mat, step_mat, decay_mat, skip, cols,
+    out, out_spec, norm_of=None,
+):
     heads = step_mat.shape[0]
     size = write_mat.shape[0]
     blocks = step_mat.shape[1] // BLOCK
@@ -319,28 +397,37 @@
     wide = pl.BlockSpec((size, BLOCK), lambda b: (0, b))
     thin = pl.BlockSpec((heads, BLOCK), lambda b: (0, b))
     rows = pl.BlockSpec((1, BLOCK, features), lambda b: (b, 0, 0))
-    end_state, totals = pl.pallas_call(
-        functools.partial(states_kernel, heads),
+    params = pltpu.CompilerParams(vmem_limit_bytes=VMEM_BYTES)
+    scale_of, extra, extra_specs = None, (), []
+    shapes = [
+        jax.ShapeDtypeStruct((heads, size, width), F32),
+        jax.ShapeDtypeStruct((heads, LANES), F32),
+    ]
+    specs = [
+        pl.BlockSpec((heads, size, width), lambda b: (0, 0, 0)),
+        pl.BlockSpec((heads, LANES), lambda b: (0, 0)),
+    ]
+    if norm_of is not None:
+        scale_of, extra, extra_specs = norm_of
+        shapes.append(jax.ShapeDtypeStruct((blocks, BLOCK, features), BF16))
+        specs.append(rows)
+    made = pl.pallas_call(
+        functools.partial(states_kernel, heads, scale_of),
         grid=(blocks,),
-        out_shape=(
-            jax.ShapeDtypeStruct((heads, size, width), F32),
-            jax.ShapeDtypeStruct((heads, LANES), F32),
-        ),
-        in_specs=[x_spec, wide, thin, thin],
-        out_specs=(
-            pl.BlockSpec((heads, size, width), lambda b: (0, 0, 0)),
-            pl.BlockSpec((heads, LANES), lambda b: (0, 0)),
-        ),
+        out_shape=shapes,
+        in_specs=[*extra_specs, x_spec, wide, thin, thin],
+        out_specs=specs,
+        compiler_params=params,
         name=f"states_{number}",
-    )(inputs, write_mat, step_mat, decay_mat)
-    prior = carried_state(seq, end_state, totals, number)
-    gated, squares = pl.pallas_call(
-        functools.partial(main_kernel, heads),
+    )(*extra, inputs, write_mat, step_mat, decay_mat)
+    prior = carried_state(seq, made[0], made[1], number)
+    if norm_of is not None:
+        inputs, x_spec = made[2], rows
+    depth = -(-blocks // 8) * 8
+    return pl.pallas_call(
+        functools.partial(main_kernel, heads, cols),
         grid=(blocks,),
-        out_shape=(
-            jax.ShapeDtypeStruct((blocks, BLOCK, features), BF16),
-            jax.ShapeDtypeStruct((blocks, 8, BLOCK), F32),
-        ),
+        out_shape=(out, jax.ShapeDtypeStruct((depth, BLOCK), F32)),
         in_specs=[
             pl.BlockSpec(memory_space=pltpu.SMEM),
             x_spec,
@@ -351,43 +438,11 @@
             thin,
             pl.BlockSpec((heads, size, width), lambda b: (0, 0, 0)),
         ],
-        out_specs=(rows, pl.BlockSpec((1, 8, BLOCK), lambda b: (b, 0, 0))),
+        out_specs=(out_spec, pl.BlockSpec((depth, BLOCK), lambda b: (0, 0))),
         scratch_shapes=[pltpu.VMEM((heads, size, width), F32)],
-        compiler_params=pltpu.CompilerParams(vmem_limit_bytes=VMEM_BYTES),
+        compiler_params=params,
         name=f"main_{number}",
     )(skip, inputs, gate, write_mat, read_mat, step_mat, decay_mat, prior)
-    whole = pl.BlockSpec(memory_space=pltpu.VMEM)
-    squares = pl.pallas_call(
-        functools.partial(sum_kernel, head),
-        out_shape=jax.ShapeDtypeStruct(squares.shape, F32),
-        in_specs=[whole],
-        out_specs=whole,
-        scratch_shapes=[
-            pltpu.VMEM((head - 1,) + squares.shape, F32),
-            pltpu.SemaphoreType.DMA((head - 1,)),
-            pltpu.SemaphoreType.DMA((head - 1,)),
-        ],
-        compiler_params=comm_params(number + 2),
-        name=f"squares_{number}",
-    )(squares)
-    return gated, squares
-
-
-def normalise(head, gated, squares, gain, cols, out_shape, out_spec, number):
-    features = gated.shape[-1]
-    return pl.pallas_call(
-        functools.partial(norm_kernel, features * head, cols),
-        grid=(gated.shape[0],),
-        out_shape=jax.ShapeDtypeStruct(out_shape, BF16),
-        in_specs=[
-            pl.BlockSpec((1, BLOCK, features), lambda b: (b, 0, 0)),
-            pl.BlockSpec((1, 8, BLOCK), lambda b: (b, 0, 0)),
-            pl.BlockSpec((1, features), lambda b: (0, 0)),
-        ],
-        out_specs=out_spec,
-        compiler_params=pltpu.CompilerParams(vmem_limit_bytes=VMEM_BYTES),
-        name=f"norm_{number}",
-    )(gated, squares, gain.reshape(1, features))
 
 
 def body(
@@ -401,41 +456,85 @@
     all_rows = grid_rows * seq
     per_col = all_rows // BLOCK
     slabs = BLOCK // grid_rows
-
-    first = layer(
-        seq, head, 0, tokens_in.reshape(blocks, BLOCK, features),
-        pl.BlockSpec((1, BLOCK, features), lambda b: (b, 0, 0)),
+    inner = features * head
+    dma = pltpu.SemaphoreType.DMA
+    anywhere = pl.BlockSpec(memory_space=pl.ANY)
+    whole = pl.BlockSpec(memory_space=pltpu.VMEM)
+    rows = pl.BlockSpec((1, BLOCK, features), lambda b: (b, 0, 0))
+
+    gated, squares = layer(
+        seq, 0, tokens_in.reshape(blocks, BLOCK, features), rows,
         gate_rows.reshape(blocks, BLOCK, features),
-        write_rows, read_rows, step_rows, decay_rows, skip_rows,
-    )
-    hidden = normalise(
-        head, *first, norm_rows, grid_cols, (seq, local_cols, grid_rows, features),
-        pl.BlockSpec((seq, local_cols, high, features), lambda b: (0, 0, b, 0)), 0,
-    )
-    anywhere = pl.BlockSpec(memory_space=pl.ANY)
-    dma = pltpu.SemaphoreType.DMA
-    hidden = pl.pallas_call(
-        functools.partial(trade_kernel, seq),
-        out_shape=jax.ShapeDtypeStruct(hidden.shape, BF16),
-        in_specs=[anywhere],
-        out_specs=anywhere,
-        scratch_shapes=[dma((seq - 1,)), dma((seq - 1,)), dma(())],
-        compiler_params=comm_params(4),
+        write_rows, read_rows, step_rows, decay_rows, skip_rows, grid_cols,
+        jax.ShapeDtypeStruct((seq, local_cols, grid_rows, features), BF16),
+        pl.BlockSpec((seq, local_cols, high, features), lambda b: (0, 0, b, 0)),
+    )
+    depth = squares.shape[0]
+    hidden, scales = pl.pallas_call(
+        functools.partial(trade_kernel, seq, head, inner),
+        out_shape=(
+            jax.ShapeDtypeStruct(gated.shape, BF16),
+            jax.ShapeDtypeStruct((seq * depth, BLOCK), F32),
+        ),
+        in_specs=[anywhere, whole],
+        out_specs=(anywhere, whole),
+        scratch_shapes=[
+            pltpu.VMEM((head - 1,) + squares.shape, F32),
+            pltpu.VMEM(squares.shape, F32),
+            dma((head - 1,)), dma((head - 1,)),
+            dma((seq - 1,)), dma((seq - 1,)),
+            dma((seq - 1,)), dma((seq - 1,)), dma(()),
+        ],
+        compiler_params=comm_params(2),
         name="trade",
-    )(hidden)
+    )(gated, squares)
     gate = jnp.transpose(gate_cols, (1, 0, 2)).reshape(local_cols * per_col, BLOCK, features)
-    second = layer(
-        seq, head, 1, hidden,
+    gated, squares = layer(
+        seq, 1, hidden,
         pl.BlockSpec(
             (slabs, 1, grid_rows, features), lambda b: (b % per_col, b // per_col, 0, 0)
         ),
-        gate, write_cols, read_cols, step_cols, decay_cols, skip_cols,
-    )
-    result = normalise(
-        head, *second, norm_cols, 1, (local_cols * per_col, BLOCK, features),
-        pl.BlockSpec((1, BLOCK, features), lambda b: (b, 0, 0)), 1,
-    )
-    return jnp.transpose(result.reshape(local_cols, all_rows, features), (1, 0, 2))
+        gate, write_cols, read_cols, step_cols, decay_cols, skip_cols, 1,
+        jax.ShapeDtypeStruct((local_cols * per_col, BLOCK, features), F32), rows,
+        (
+            functools.partial(column_scale, local_cols, per_col, grid_rows, grid_cols),
+            (lax.axis_index("seq").reshape(1), scales, norm_rows.reshape(1, features)),
+            [
+                pl.BlockSpec(memory_space=pltpu.SMEM),
+                pl.BlockSpec((slabs * depth, BLOCK), lambda b: (b % per_col, 0)),
+                pl.BlockSpec((1, features), lambda b: (0, 0)),
+            ],
+        ),
+    )
+    squares = pl.pallas_call(
+        functools.partial(sum_kernel, head),
+        out_shape=jax.ShapeDtypeStruct(squares.shape, F32),
+        in_specs=[whole],
+        out_specs=whole,
+        scratch_shapes=[
+            pltpu.VMEM((head - 1,) + squares.shape, F32), dma((head - 1,)), dma((head - 1,)),
+        ],
+        compiler_params=comm_params(3),
+        name="squares",
+    )(squares)
+    part = BLOCK // local_cols
+    out_shape, out_spec = (all_rows, local_cols, features), (part, local_cols, features)
+    if local_cols == 1:
+        out_shape, out_spec = (all_rows, features), (part, features)
+    result = pl.pallas_call(
+        functools.partial(norm_kernel, inner, per_col),
+        grid=(all_rows // part,),
+        out_shape=jax.ShapeDtypeStruct(out_shape, BF16),
+        in_specs=[
+            pl.BlockSpec((local_cols, part, features), lambda q: (0, q, 0)),
+            pl.BlockSpec(squares.shape, lambda q: (0, 0)),
+            pl.BlockSpec((1, features), lambda q: (0, 0)),
+        ],
+        out_specs=pl.BlockSpec(out_spec, lambda q: (q,) + (0,) * (len(out_spec) - 1)),
+        compiler_params=pltpu.CompilerParams(vmem_limit_bytes=VMEM_BYTES),
+        name="norm",
+    )(gated.reshape(local_cols, all_rows, features), squares, norm_cols.reshape(1, features))
+    return result.reshape(all_rows, local_cols, features)
 
 
 def solution(mesh):

time: 183 us -> 178 us (0.973)
  local copies, waits for them, and re-layouts: 9.43 us -> 3.47 us
    transpose x1 -> x0, local copies, waits for them, and re-layouts: 5.98 us -> none  [body(): jnp.transpose(result.reshape(local_cols, all_rows, features), (1, 0, 2))]
    pallas_call x9 -> x7, Pallas kernels: 133 us -> 136 us  [the longest x1 79 us: body(): pl.pallas_call(functools.partial(trade_kernel, seq, head, inner), out_sha...]
    pallas_call x2, Pallas kernels: 39.1 us -> 36.2 us  [carried_state(): pl.pallas_call(functools.partial(prior_kernel, seq), out_shape=jax.ShapeD...]
where the time goes in v2:
time: 178 us; the launch traced here: 176 us
  Pallas kernels  173 us (97%)
  local copies, waits for them, and re-layouts  3.47 us (2%)
    pallas_call x1, Pallas kernels, body(): pl.pallas_call(functools.partial(trade_kernel, seq, head, inner), out_sha...  79 us
    pallas_call x2, Pallas kernels, carried_state(): pl.pallas_call(functools.partial(prior_kernel, seq), out_shape=jax.ShapeD...  36.2 us
    pallas_call x2, Pallas kernels, layer(): pl.pallas_call(functools.partial(main_kernel, heads, cols), grid=(blocks,...  32.5 us
    pallas_call x2, Pallas kernels, layer(): pl.pallas_call(functools.partial(states_kernel, heads, scale_of), grid=(b...  11.6 us
    pallas_call x1, Pallas kernels, body(): pl.pallas_call(functools.partial(norm_kernel, inner, per_col), grid=(all_...  8.29 us
    pallas_call x1, Pallas kernels, body(): pl.pallas_call(functools.partial(sum_kernel, head), out_shape=jax.ShapeDt...  5 us

profile of v2, /device:TPU:0, one launch (start us, length us, event | category | flops | bytes accessed | tf_op | source)
XLA Modules:
  0.0 176.1 jit_solution(15187364182549400055)
XLA Ops:
  0.0 5.1 %states_0.1 = (f32[12,64,128]{2,1,0:T(8,128)}, f32[12,128]{1,0:T(8,128)}) custom-call(bf16[4,256,1536]{2,1,0:T(8,128)(2,1)} %bitcast.7, bf16[64,1024]{1,0:T(8,128)(2,1)} %write_ref.2, f32[12,1024]{1,0:T(8,128)} %step_ref.2, f32[12,1024]{1,0:T(8,128)} %decay_ref.2), custom_call_target="tpu_custom_call" | custom-call | tf_op jit(solution)/shard_map/states_0/pallas_call | solution.py:414
  5.1 21.7 %prior_0.1.prior_ref = f32[12,64,128]{2,1,0:T(8,128)} custom-call(f32[12,64,128]{2,1,0:T(8,128)} %get-tuple-element.16.end_ref, f32[12,128]{1,0:T(8,128)} %get-tuple-element.17.total_ref), custom_call_target="tpu_custom_call" | custom-call | tf_op jit(solution)/shard_map/prior_0/pallas_call | solution.py:360
  26.8 19.1 %main_0.1 = (bf16[8,4,32,1536]{3,2,1,0:T(8,128)(2,1)}, f32[8,256]{1,0:T(8,128)}) custom-call(f32[12]{0:T(128)} %skip_ref.2, bf16[4,256,1536]{2,1,0:T(8,128)(2,1)} %bitcast.8, bf16[4,256,1536]{2,1,0:T(8,128)(2,1)} %bitcast.9, bf16[64,1024]{1,0:T(8,128)(2,1)} %write_ref.2, bf16[64,1024]{1,0:T(8,128)(2,1)} %read_ref.2, f32[12,1024]{1,0:T(8,128)} %step_ref.2, ...), custom_call_target="tpu_custom_call" | custom-call | tf_op jit(solution)/shard_map/main_0/pallas_call | solution.py:427
  45.9 0.0 copy-start.1
  45.9 0.0 copy-start
  45.9 79.0 %trade.1 = (bf16[8,4,32,1536]{3,2,1,0:T(8,128)(2,1)}, f32[64,256]{1,0:T(8,128)}) custom-call(bf16[8,4,32,1536]{3,2,1,0:T(8,128)(2,1)} %get-tuple-element.18.own_ref, f32[8,256]{1,0:T(8,128)} %get-tuple-element.19.squares_ref), custom_call_target="tpu_custom_call" | custom-call | tf_op jit(solution)/shard_map/trade/pallas_call | solution.py:473
  124.9 0.0 copy-done.1
  124.9 0.6 reshape.18.refs_2_
  125.5 6.5 %states_1.1 = (f32[12,64,128]{2,1,0:T(8,128)}, f32[12,128]{1,0:T(8,128)}, bf16[4,256,1536]{2,1,0:T(8,128)(2,1)}) custom-call(s32[1]{0:T(128)} %bitcast.refs_0_, f32[64,256]{1,0:T(8,128)} %get-tuple-element.20.refs_1_, f32[1,1536]{1,0:T(1,128)} %reshape.18.refs_2_, bf16[8,4,32,1536]{3,2,1,0:T(8,128)(2,1)} %get-tuple-element.21.refs_3_, ...), custom_call_target="tpu_custom_call" | custom-call | tf_op jit(solution)/shard_map/states_1/pallas_call | solution.py:414
  132.0 14.6 %prior_1.1.prior_ref = f32[12,64,128]{2,1,0:T(8,128)} custom-call(f32[12,64,128]{2,1,0:T(8,128)} %get-tuple-element.23.end_ref, f32[12,128]{1,0:T(8,128)} %get-tuple-element.24.total_ref), custom_call_target="tpu_custom_call" | custom-call | tf_op jit(solution)/shard_map/prior_1/pallas_call | solution.py:360
  146.6 0.0 copy-done
  146.6 2.3 %copy.18 = bf16[256,4,1536]{2,0,1:T(8,128)(2,1)} copy(bf16[256,4,1536]{2,1,0:T(4,128)(2,1)S(1)} %copy-done) | data formatting | bytes 6291456 | tf_op args[2]
  148.9 0.0 copy-start.2
  148.9 13.3 %main_1.1 = (f32[4,256,1536]{2,1,0:T(8,128)}, f32[8,256]{1,0:T(8,128)}) custom-call(f32[12]{0:T(128)} %skip_ref.3, bf16[4,256,1536]{2,1,0:T(8,128)(2,1)} %get-tuple-element.22.x_ref, bf16[4,256,1536]{2,1,0:T(8,128)(2,1)} %bitcast.6, bf16[64,1024]{1,0:T(8,128)(2,1)} %write_ref.3, bf16[64,1024]{1,0:T(8,128)(2,1)} %read_ref.3, f32[12,1024]{1,0:T(8,128)} %step_ref.3, ...), custom_call_target="tpu_custom_call" | custom-call | tf_op jit(solution)/shard_map/main_1/pallas_call | solution.py:427
  162.2 5.0 %squares.1.squares_ref = f32[8,256]{1,0:T(8,128)} custom-call(f32[8,256]{1,0:T(8,128)} %get-tuple-element.26.own_ref), custom_call_target="tpu_custom_call" | custom-call | tf_op jit(solution)/shard_map/squares/pallas_call | solution.py:509
  167.2 0.0 copy-done.2
  167.3 0.6 reshape.19.gain_ref
  167.9 8.3 %norm.1 = bf16[256,4,1536]{2,1,0:T(4,128)(2,1)} custom-call(f32[4,256,1536]{2,1,0:T(8,128)} %get-tuple-element.25.gated_ref, f32[8,256]{1,0:T(8,128)} %squares.1.squares_ref, f32[1,1536]{1,0:T(1,128)} %reshape.19.gain_ref), custom_call_target="tpu_custom_call" | custom-call | tf_op jit(solution)/shard_map/norm/pallas_call | solution.py:524
Async XLA Ops:
  45.9 79.0 %copy-start.1 = (f32[1536]{0:T(1024)S(1)}, f32[1536]{0:T(1024)}, u32[]{:S(2)}) copy-start(f32[1536]{0:T(1024)} %param.23) | copy-start | bytes 18436
  45.9 100.7 %copy-start = (bf16[256,4,1536]{2,1,0:T(4,128)(2,1)S(1)}, bf16[256,4,1536]{2,1,0:T(4,128)(2,1)}, u32[]{:S(2)}) copy-start(bf16[256,4,1536]{2,1,0:T(4,128)(2,1)} %param.17) | copy-start | bytes 9437188
  148.9 18.3 %copy-start.2 = (f32[1536]{0:T(1024)S(1)}, f32[1536]{0:T(1024)}, u32[]{:S(2)}) copy-start(f32[1536]{0:T(1024)} %param.29) | copy-start | bytes 18436

commit v3 on v2

--- a/solution.py
+++ b/solution.py
@@ -85,7 +85,7 @@
 
 def main_kernel(
     heads, cols, skip_ref, x_ref, gate_ref, write_ref, read_ref, step_ref, decay_ref, prior_ref,
-    gated_ref, squares_ref, state,
+    gated_ref, squares_ref, state, turned,
 ):
     @pl.when(pl.program_id(0) == 0)
     def _():
@@ -108,34 +108,43 @@
     squares = jnp.zeros((BLOCK, LANES), F32)
     read_twice = jnp.concatenate([read, read], axis=0)
     high = BLOCK // cols
-    to = iota((BLOCK, BLOCK), 0)
-    chosen = ((to % high) * cols + to // high == iota((BLOCK, BLOCK), 1)).astype(BF16)
     for h in range(heads):
         lanes = slice(h * LANES, (h + 1) * LANES)
         own = tokens[:, lanes]
         spread = jnp.minimum(across[:, h : h + 1] - cumulative[h : h + 1], 0.0)
         mixing = (jnp.exp2(spread) * scores * step[h : h + 1]).astype(BF16)
         held = state[h]
-        out = contract(mixing, own, ((1,), (0,)))
-        coarse = held.astype(BF16)
-        fine = (held - coarse.astype(F32)).astype(BF16)
-        parts = jnp.concatenate([coarse, fine], axis=0)
-        out += lifting[:, h : h + 1] * contract(read_twice, parts, ((0,), (0,)))
+        loaded = (write32 * weights[h : h + 1]).astype(BF16)
+        both = contract(jnp.concatenate([mixing, loaded], axis=0), own, ((1,), (0,)))
+        out = both[:BLOCK]
+        if h % 2 == 0:
+            pair = jnp.concatenate([held] + ([state[h + 1]] if h + 1 < heads else []), axis=1)
+            coarse = pair.astype(BF16)
+            fine = (pair - coarse.astype(F32)).astype(BF16)
+            parts = jnp.concatenate([coarse, fine], axis=0)
+            from_state = contract(read_twice, parts, ((0,), (0,)))
+        side = (h % 2) * LANES
+        out += lifting[:, h : h + 1] * from_state[:, side : side + LANES]
         out += skip_ref[h] * own.astype(F32)
         gate = gate_ref[0, :, lanes].astype(F32)
         gated = out * (gate / (1.0 + jnp.exp2(gate * -LOG2E)))
         squares += gated * gated
         if cols > 1:
-            moved = contract(chosen, gated.astype(BF16), ((1,), (0,)))
-            gated_ref[:, :, :, lanes] = moved.reshape(gated_ref.shape[:3] + (LANES,)).astype(BF16)
+            near = gated_ref.shape[1]
+            slot = turned.at[h % 2]
+            slot[...] = gated
+            for c in range(cols):
+                gated_ref[c // near, c % near, :, lanes] = slot[
+                    pl.ds(c, high, stride=cols), :
+                ].astype(BF16)
         else:
             gated_ref[0, :, lanes] = gated
-        state[h] = fade[h : h + 1] * held + head_state(write32, weights[h : h + 1], own)
+        state[h] = fade[h : h + 1] * held + both[BLOCK:]
     row = contract(jnp.ones((8, LANES), F32), squares, ((1,), (1,)), HIGHEST)
     squares_ref[pl.ds(pl.program_id(0), 1), :] = row[:1]
 
 
-def norm_kernel(inner, per_col, gated_ref, squares_ref, gain_ref, out_ref):
+def norm_kernel(inner, per_col, gated_ref, squares_ref, gain_ref, out_ref, turned):
     cols, rows, features = gated_ref.shape
     square = (BLOCK, BLOCK)
     start = pl.program_id(0) * rows
@@ -144,16 +153,16 @@
     block = (iota(sums.shape, 0) // rows) * per_col + start // BLOCK
     sums = jnp.sum(jnp.where(iota(sums.shape, 1) == block, sums, 0.0), axis=1, keepdims=True)
     scaled = lax.rsqrt(sums / inner + EPSILON)
-    chosen = ((iota(square, 0) % cols) * rows + iota(square, 0) // cols == iota(square, 1)).astype(BF16)
     for at in range(0, features, LANES):
         lanes = slice(at, at + LANES)
         result = gated_ref[:, :, lanes].reshape(BLOCK, LANES) * scaled * gain_ref[:, lanes]
-        result = result.astype(BF16)
         if cols > 1:
-            moved = contract(chosen, result, ((1,), (0,)))
-            out_ref[:, :, lanes] = moved.reshape(rows, cols, LANES).astype(BF16)
+            slot = turned.at[at // LANES % 2]
+            for c in range(cols):
+                slot[pl.ds(c, rows, stride=cols), :] = result[c * rows : (c + 1) * rows]
+            out_ref[:, :, lanes] = slot[...].reshape(rows, cols, LANES).astype(BF16)
         else:
-            out_ref[:, lanes] = result
+            out_ref[:, lanes] = result.astype(BF16)
 
 
 def greet(axes):
@@ -439,7 +448,9 @@
             pl.BlockSpec((heads, size, width), lambda b: (0, 0, 0)),
         ],
         out_specs=(out_spec, pl.BlockSpec((depth, BLOCK), lambda b: (0, 0))),
-        scratch_shapes=[pltpu.VMEM((heads, size, width), F32)],
+        scratch_shapes=[
+            pltpu.VMEM((heads, size, width), F32), pltpu.VMEM((2, BLOCK, width), F32)
+        ],
         compiler_params=params,
         name=f"main_{number}",
     )(skip, inputs, gate, write_mat, read_mat, step_mat, decay_mat, prior)
@@ -531,6 +542,7 @@
             pl.BlockSpec((1, features), lambda q: (0, 0)),
         ],
         out_specs=pl.BlockSpec(out_spec, lambda q: (q,) + (0,) * (len(out_spec) - 1)),
+        scratch_shapes=[pltpu.VMEM((2, BLOCK, LANES), F32)],
         compiler_params=pltpu.CompilerParams(vmem_limit_bytes=VMEM_BYTES),
         name="norm",
     )(gated.reshape(local_cols, all_rows, features), squares, norm_cols.reshape(1, features))

time: 178 us -> 174 us (0.978)
  Pallas kernels: 173 us -> 169 us
    pallas_call x2, Pallas kernels: 32.5 us -> 30.2 us  [layer(): pl.pallas_call(functools.partial(main_kernel, heads, cols), grid=(blocks,...]
where the time goes in v3:
time: 174 us; the launch traced here: 172 us
  Pallas kernels  169 us (97%)
  local copies, waits for them, and re-layouts  3.47 us (2%)
    pallas_call x1, Pallas kernels, body(): pl.pallas_call(functools.partial(trade_kernel, seq, head, inner), out_sha...  78.9 us
    pallas_call x2, Pallas kernels, carried_state(): pl.pallas_call(functools.partial(prior_kernel, seq), out_shape=jax.ShapeD...  36.2 us
    pallas_call x2, Pallas kernels, layer(): pl.pallas_call(functools.partial(main_kernel, heads, cols), grid=(blocks,...  30.2 us
    pallas_call x2, Pallas kernels, layer(): pl.pallas_call(functools.partial(states_kernel, heads, scale_of), grid=(b...  11.6 us
    pallas_call x1, Pallas kernels, body(): pl.pallas_call(functools.partial(norm_kernel, inner, per_col), grid=(all_...  6.68 us
    pallas_call x1, Pallas kernels, body(): pl.pallas_call(functools.partial(sum_kernel, head), out_shape=jax.ShapeDt...  5 us

profile of v3, /device:TPU:0, one launch (start us, length us, event | category | flops | bytes accessed | tf_op | source)
XLA Modules:
  0.0 172.3 jit_solution(7745010544384975898)
XLA Ops:
  0.0 5.1 %states_0.1 = (f32[12,64,128]{2,1,0:T(8,128)}, f32[12,128]{1,0:T(8,128)}) custom-call(bf16[4,256,1536]{2,1,0:T(8,128)(2,1)} %bitcast.7, bf16[64,1024]{1,0:T(8,128)(2,1)} %write_ref.2, f32[12,1024]{1,0:T(8,128)} %step_ref.2, f32[12,1024]{1,0:T(8,128)} %decay_ref.2), custom_call_target="tpu_custom_call" | custom-call | tf_op jit(solution)/shard_map/states_0/pallas_call | solution.py:423
  5.1 21.7 %prior_0.1.prior_ref = f32[12,64,128]{2,1,0:T(8,128)} custom-call(f32[12,64,128]{2,1,0:T(8,128)} %get-tuple-element.16.end_ref, f32[12,128]{1,0:T(8,128)} %get-tuple-element.17.total_ref), custom_call_target="tpu_custom_call" | custom-call | tf_op jit(solution)/shard_map/prior_0/pallas_call | solution.py:369
  26.8 17.1 %main_0.1 = (bf16[8,4,32,1536]{3,2,1,0:T(8,128)(2,1)}, f32[8,256]{1,0:T(8,128)}) custom-call(f32[12]{0:T(128)} %skip_ref.2, bf16[4,256,1536]{2,1,0:T(8,128)(2,1)} %bitcast.8, bf16[4,256,1536]{2,1,0:T(8,128)(2,1)} %bitcast.9, bf16[64,1024]{1,0:T(8,128)(2,1)} %write_ref.2, bf16[64,1024]{1,0:T(8,128)(2,1)} %read_ref.2, f32[12,1024]{1,0:T(8,128)} %step_ref.2, ...), custom_call_target="tpu_custom_call" | custom-call | tf_op jit(solution)/shard_map/main_0/pallas_call | solution.py:436
  43.9 0.0 copy-start.1
  43.9 0.0 copy-start
  43.9 78.9 %trade.1 = (bf16[8,4,32,1536]{3,2,1,0:T(8,128)(2,1)}, f32[64,256]{1,0:T(8,128)}) custom-call(bf16[8,4,32,1536]{3,2,1,0:T(8,128)(2,1)} %get-tuple-element.18.own_ref, f32[8,256]{1,0:T(8,128)} %get-tuple-element.19.squares_ref), custom_call_target="tpu_custom_call" | custom-call | tf_op jit(solution)/shard_map/trade/pallas_call | solution.py:484
  122.9 0.0 copy-done.1
  122.9 0.6 reshape.18.refs_2_
  123.5 6.5 %states_1.1 = (f32[12,64,128]{2,1,0:T(8,128)}, f32[12,128]{1,0:T(8,128)}, bf16[4,256,1536]{2,1,0:T(8,128)(2,1)}) custom-call(s32[1]{0:T(128)} %bitcast.refs_0_, f32[64,256]{1,0:T(8,128)} %get-tuple-element.20.refs_1_, f32[1,1536]{1,0:T(1,128)} %reshape.18.refs_2_, bf16[8,4,32,1536]{3,2,1,0:T(8,128)(2,1)} %get-tuple-element.21.refs_3_, ...), custom_call_target="tpu_custom_call" | custom-call | tf_op jit(solution)/shard_map/states_1/pallas_call | solution.py:423
  130.0 14.6 %prior_1.1.prior_ref = f32[12,64,128]{2,1,0:T(8,128)} custom-call(f32[12,64,128]{2,1,0:T(8,128)} %get-tuple-element.23.end_ref, f32[12,128]{1,0:T(8,128)} %get-tuple-element.24.total_ref), custom_call_target="tpu_custom_call" | custom-call | tf_op jit(solution)/shard_map/prior_1/pallas_call | solution.py:369
  144.6 0.0 copy-done
  144.6 2.3 %copy.18 = bf16[256,4,1536]{2,0,1:T(8,128)(2,1)} copy(bf16[256,4,1536]{2,1,0:T(4,128)(2,1)S(1)} %copy-done) | data formatting | bytes 6291456 | tf_op args[2]
  146.9 0.0 copy-start.2
  146.9 13.1 %main_1.1 = (f32[4,256,1536]{2,1,0:T(8,128)}, f32[8,256]{1,0:T(8,128)}) custom-call(f32[12]{0:T(128)} %skip_ref.3, bf16[4,256,1536]{2,1,0:T(8,128)(2,1)} %get-tuple-element.22.x_ref, bf16[4,256,1536]{2,1,0:T(8,128)(2,1)} %bitcast.6, bf16[64,1024]{1,0:T(8,128)(2,1)} %write_ref.3, bf16[64,1024]{1,0:T(8,128)(2,1)} %read_ref.3, f32[12,1024]{1,0:T(8,128)} %step_ref.3, ...), custom_call_target="tpu_custom_call" | custom-call | tf_op jit(solution)/shard_map/main_1/pallas_call | solution.py:436
  160.0 5.0 %squares.1.squares_ref = f32[8,256]{1,0:T(8,128)} custom-call(f32[8,256]{1,0:T(8,128)} %get-tuple-element.26.own_ref), custom_call_target="tpu_custom_call" | custom-call | tf_op jit(solution)/shard_map/squares/pallas_call | solution.py:520
  165.0 0.0 copy-done.2
  165.0 0.6 reshape.19.gain_ref
  165.6 6.7 %norm.1 = bf16[256,4,1536]{2,1,0:T(4,128)(2,1)} custom-call(f32[4,256,1536]{2,1,0:T(8,128)} %get-tuple-element.25.gated_ref, f32[8,256]{1,0:T(8,128)} %squares.1.squares_ref, f32[1,1536]{1,0:T(1,128)} %reshape.19.gain_ref), custom_call_target="tpu_custom_call" | custom-call | tf_op jit(solution)/shard_map/norm/pallas_call | solution.py:535
Async XLA Ops:
  43.9 79.0 %copy-start.1 = (f32[1536]{0:T(1024)S(1)}, f32[1536]{0:T(1024)}, u32[]{:S(2)}) copy-start(f32[1536]{0:T(1024)} %param.23) | copy-start | bytes 18436
  43.9 100.7 %copy-start = (bf16[256,4,1536]{2,1,0:T(4,128)(2,1)S(1)}, bf16[256,4,1536]{2,1,0:T(4,128)(2,1)}, u32[]{:S(2)}) copy-start(bf16[256,4,1536]{2,1,0:T(4,128)(2,1)} %param.17) | copy-start | bytes 9437188
  146.9 18.1 %copy-start.2 = (f32[1536]{0:T(1024)S(1)}, f32[1536]{0:T(1024)}, u32[]{:S(2)}) copy-start(f32[1536]{0:T(1024)} %param.29) | copy-start | bytes 18436

commit v4 on v3

--- a/solution.py
+++ b/solution.py
@@ -92,6 +92,16 @@
         state[...] = prior_ref[...]
         squares_ref[...] = jnp.zeros_like(squares_ref)
 
+    main_block(
+        heads, cols, pl.program_id(0), skip_ref, x_ref, gate_ref, write_ref, read_ref, step_ref,
+        decay_ref, gated_ref, squares_ref, state, turned,
+    )
+
+
+def main_block(
+    heads, cols, at, skip_ref, x_ref, gate_ref, write_ref, read_ref, step_ref, decay_ref,
+    gated_ref, squares_ref, state, turned,
+):
     decay = decay_ref[...] * LOG2E
     step = step_ref[...]
     cumulative, total = block_sums(decay)
@@ -141,7 +151,7 @@
             gated_ref[0, :, lanes] = gated
         state[h] = fade[h : h + 1] * held + both[BLOCK:]
     row = contract(jnp.ones((8, LANES), F32), squares, ((1,), (1,)), HIGHEST)
-    squares_ref[pl.ds(pl.program_id(0), 1), :] = row[:1]
+    squares_ref[pl.ds(at, 1), :] = row[:1]
 
 
 def norm_kernel(inner, per_col, gated_ref, squares_ref, gain_ref, out_ref, turned):
@@ -166,6 +176,11 @@
 
 
 def greet(axes):
+    greet_signal(axes)
+    greet_wait(axes)
+
+
+def greet_signal(axes):
     barrier = pltpu.get_barrier_semaphore()
     for axis, count in axes:
         me = lax.axis_index(axis)
@@ -173,7 +188,12 @@
             pl.semaphore_signal(
                 barrier, inc=1, device_id={axis: lax.rem(me + hop, count)}, device_id_type=MESH
             )
-    pl.semaphore_wait(barrier, sum(count - 1 for _, count in axes))
+
+
+def greet_wait(axes):
+    pl.semaphore_wait(
+        pltpu.get_barrier_semaphore(), sum(count - 1 for _, count in axes)
+    )
 
 
 def head_sum(count, own_ref, held, send_sems, recv_sems):
@@ -204,31 +224,77 @@
 
 
 def trade_kernel(
-    count, heads, inner, own_ref, squares_ref, out_ref, scales_ref, held, scale, sum_send,
-    sum_recv, scale_send, scale_recv, send_sems, recv_sems, local_sem,
+    count, head_count, inner, heads, cols, skip_ref, x_hbm, gate_hbm, write_ref, read_ref,
+    step_ref, decay_ref, prior_ref, out_ref, scales_ref, x_ref, gate_ref, gated, squares, state,
+    turned, held, scale, load_sems, sum_send, sum_recv, scale_send, scale_recv, send_sems,
+    recv_sems, local_sems,
 ):
-    greet((("seq", count), ("head", heads)))
+    axes = (("seq", count), ("head", head_count))
+    blocks, features = x_ref.shape[0], x_ref.shape[-1]
+    high = gated.shape[3]
     me = lax.axis_index("seq")
-    copies = []
-    for hop in range(count // 2, count // 2 + count - 1):
-        ahead = 1 + (hop - 1) % (count - 1)
+    greet_signal(axes)
+
+    def load(b):
+        return (
+            pltpu.make_async_copy(x_hbm.at[b], x_ref.at[b], load_sems.at[0, b]),
+            pltpu.make_async_copy(gate_hbm.at[b], gate_ref.at[b], load_sems.at[1, b]),
+        )
+
+    for b in range(blocks):
+        for copy in load(b):
+            copy.start()
+    state[...] = prior_ref[...]
+    squares[...] = jnp.zeros_like(squares)
+
+    def compute(b):
+        for copy in load(b):
+            copy.wait()
+        span = pl.ds(pl.multiple_of(b * BLOCK, BLOCK), BLOCK)
+        one = pl.ds(b, 1)
+        main_block(
+            heads, cols, b, skip_ref, x_ref.at[one], gate_ref.at[one], write_ref.at[:, span],
+            read_ref.at[:, span], step_ref.at[:, span], decay_ref.at[:, span], gated.at[b],
+            squares, state, turned,
+        )
+
+    def rows_of(b):
+        return out_ref.at[me, :, pl.ds(pl.multiple_of(b * high, high), high)]
+
+    def send(b, ahead):
         to = lax.rem(me + ahead, count)
-        copy = pltpu.make_async_remote_copy(
-            src_ref=own_ref.at[to],
-            dst_ref=out_ref.at[me],
-            send_sem=send_sems.at[ahead - 1],
-            recv_sem=recv_sems.at[ahead - 1],
+        return pltpu.make_async_remote_copy(
+            src_ref=gated.at[b, to],
+            dst_ref=rows_of(b),
+            send_sem=send_sems.at[ahead - 1, b],
+            recv_sem=recv_sems.at[ahead - 1, b],
             device_id={"seq": to},
             device_id_type=MESH,
         )
-        copy.start()
-        copies.append(copy)
-    local = pltpu.make_async_copy(own_ref.at[me], out_ref.at[me], local_sem)
-    local.start()
-    total = head_sum(heads, squares_ref, held, sum_send, sum_recv)
+
+    def keep(b):
+        return pltpu.make_async_copy(gated.at[b, me], rows_of(b), local_sems.at[b])
+
+    def send_all(b):
+        for hop in range(count // 2, count // 2 + count - 1):
+            send(b, 1 + (hop - 1) % (count - 1)).start()
+        keep(b).start()
+
+    compute(0)
+    greet_wait(axes)
+    send_all(0)
+
+    def step(b, carry):
+        compute(b)
+        send_all(b)
+        return carry
+
+    lax.fori_loop(1, blocks, step, 0)
+    total = head_sum(head_count, squares, held, sum_send, sum_recv)
     scale[...] = lax.rsqrt(total / inner + EPSILON)
     depth = scale.shape[0]
     mine = pl.ds(pl.multiple_of(me * depth, depth), depth)
+    copies = []
     for hop in range(1, count):
         copy = pltpu.make_async_remote_copy(
             src_ref=scale,
@@ -241,9 +307,16 @@
         copy.start()
         copies.append(copy)
     scales_ref[mine, :] = scale[...]
-    local.wait()
     for copy in copies:
         copy.wait()
+
+    def settle(b, carry):
+        keep(b).wait()
+        for ahead in range(1, count):
+            send(b, ahead).wait()
+        return carry
+
+    lax.fori_loop(0, blocks, settle, 0)
 
 
 def prior_kernel(
@@ -396,7 +469,7 @@
 
 def layer(
     seq, number, inputs, x_spec, gate, write_mat, read_mat, step_mat, decay_mat, skip, cols,
-    out, out_spec, norm_of=None,
+    out, out_spec, norm_of=None, send=None,
 ):
     heads = step_mat.shape[0]
     size = write_mat.shape[0]
@@ -433,6 +506,8 @@
     if norm_of is not None:
         inputs, x_spec = made[2], rows
     depth = -(-blocks // 8) * 8
+    if send is not None:
+        return send(skip, inputs, gate, write_mat, read_mat, step_mat, decay_mat, prior)
     return pl.pallas_call(
         functools.partial(main_kernel, heads, cols),
         grid=(blocks,),
@@ -473,32 +548,39 @@
     whole = pl.BlockSpec(memory_space=pltpu.VMEM)
     rows = pl.BlockSpec((1, BLOCK, features), lambda b: (b, 0, 0))
 
-    gated, squares = layer(
-        seq, 0, tokens_in.reshape(blocks, BLOCK, features), rows,
-        gate_rows.reshape(blocks, BLOCK, features),
-        write_rows, read_rows, step_rows, decay_rows, skip_rows, grid_cols,
-        jax.ShapeDtypeStruct((seq, local_cols, grid_rows, features), BF16),
-        pl.BlockSpec((seq, local_cols, high, features), lambda b: (0, 0, b, 0)),
-    )
-    depth = squares.shape[0]
-    hidden, scales = pl.pallas_call(
-        functools.partial(trade_kernel, seq, head, inner),
+    heads, size = step_rows.shape[0], write_rows.shape[0]
+    width = features // heads
+    depth = -(-blocks // 8) * 8
+    send = pl.pallas_call(
+        functools.partial(trade_kernel, seq, head, inner, heads, grid_cols),
         out_shape=(
-            jax.ShapeDtypeStruct(gated.shape, BF16),
+            jax.ShapeDtypeStruct((seq, local_cols, grid_rows, features), BF16),
             jax.ShapeDtypeStruct((seq * depth, BLOCK), F32),
         ),
-        in_specs=[anywhere, whole],
+        in_specs=[pl.BlockSpec(memory_space=pltpu.SMEM), anywhere, anywhere] + [whole] * 5,
         out_specs=(anywhere, whole),
         scratch_shapes=[
-            pltpu.VMEM((head - 1,) + squares.shape, F32),
-            pltpu.VMEM(squares.shape, F32),
+            pltpu.VMEM((blocks, BLOCK, features), BF16),
+            pltpu.VMEM((blocks, BLOCK, features), BF16),
+            pltpu.VMEM((blocks, seq, local_cols, high, features), BF16),
+            pltpu.VMEM((depth, BLOCK), F32),
+            pltpu.VMEM((heads, size, width), F32),
+            pltpu.VMEM((2, BLOCK, width), F32),
+            pltpu.VMEM((head - 1, depth, BLOCK), F32),
+            pltpu.VMEM((depth, BLOCK), F32),
+            dma((2, blocks)),
             dma((head - 1,)), dma((head - 1,)),
             dma((seq - 1,)), dma((seq - 1,)),
-            dma((seq - 1,)), dma((seq - 1,)), dma(()),
+            dma((seq - 1, blocks)), dma((seq - 1, blocks)), dma((blocks,)),
         ],
         compiler_params=comm_params(2),
         name="trade",
-    )(gated, squares)
+    )
+    hidden, scales = layer(
+        seq, 0, tokens_in.reshape(blocks, BLOCK, features), rows,
+        gate_rows.reshape(blocks, BLOCK, features),
+        write_rows, read_rows, step_rows, decay_rows, skip_rows, grid_cols, None, None, None, send,
+    )
     gate = jnp.transpose(gate_cols, (1, 0, 2)).reshape(local_cols * per_col, BLOCK, features)
     gated, squares = layer(
         seq, 1, hidden,

time: 174 us -> 158 us (0.908)
  Pallas kernels: 169 us -> 154 us
    pallas_call x2 -> x1, Pallas kernels: 30.2 us -> 13.1 us  [layer(): pl.pallas_call(functools.partial(main_kernel, heads, cols), grid=(blocks,...]
    pallas_call x2, Pallas kernels: 36.2 us -> 39.4 us  [carried_state(): pl.pallas_call(functools.partial(prior_kernel, seq), out_shape=jax.ShapeD...]
where the time goes in v4:
time: 158 us; the launch traced here: 157 us
  Pallas kernels  154 us (97%)
  local copies, waits for them, and re-layouts  3.48 us (2%)
    pallas_call x1, Pallas kernels, layer(): send(skip, inputs, gate, write_mat, read_mat, step_mat, decay_mat, prior)  77.5 us
    pallas_call x2, Pallas kernels, carried_state(): pl.pallas_call(functools.partial(prior_kernel, seq), out_shape=jax.ShapeD...  39.4 us
    pallas_call x1, Pallas kernels, layer(): pl.pallas_call(functools.partial(main_kernel, heads, cols), grid=(blocks,...  13.1 us
    pallas_call x2, Pallas kernels, layer(): pl.pallas_call(functools.partial(states_kernel, heads, scale_of), grid=(b...  12 us
    pallas_call x1, Pallas kernels, body(): pl.pallas_call(functools.partial(norm_kernel, inner, per_col), grid=(all_...  6.69 us
    pallas_call x1, Pallas kernels, body(): pl.pallas_call(functools.partial(sum_kernel, head), out_shape=jax.ShapeDt...  5 us

profile of v4, /device:TPU:0, one launch (start us, length us, event | category | flops | bytes accessed | tf_op | source)
XLA Modules:
  0.0 157.2 jit_solution(17989692695086367431)
XLA Ops:
  0.0 5.1 %states_0.1 = (f32[12,64,128]{2,1,0:T(8,128)}, f32[12,128]{1,0:T(8,128)}) custom-call(bf16[4,256,1536]{2,1,0:T(8,128)(2,1)} %bitcast.7, bf16[64,1024]{1,0:T(8,128)(2,1)} %write_ref.2, f32[12,1024]{1,0:T(8,128)} %step_ref.2, f32[12,1024]{1,0:T(8,128)} %decay_ref.2), custom_call_target="tpu_custom_call" | custom-call | tf_op jit(solution)/shard_map/states_0/pallas_call | solution.py:496
  5.1 21.7 %prior_0.1.prior_ref = f32[12,64,128]{2,1,0:T(8,128)} custom-call(f32[12,64,128]{2,1,0:T(8,128)} %get-tuple-element.14.end_ref, f32[12,128]{1,0:T(8,128)} %get-tuple-element.15.total_ref), custom_call_target="tpu_custom_call" | custom-call | tf_op jit(solution)/shard_map/prior_0/pallas_call | solution.py:442
  26.8 0.0 copy-start.1
  26.8 77.5 %trade.1 = (bf16[8,4,32,1536]{3,2,1,0:T(8,128)(2,1)}, f32[64,256]{1,0:T(8,128)}) custom-call(f32[12]{0:T(128)} %skip_ref.2, bf16[4,256,1536]{2,1,0:T(8,128)(2,1)} %bitcast.8, bf16[4,256,1536]{2,1,0:T(8,128)(2,1)} %bitcast.9, bf16[64,1024]{1,0:T(8,128)(2,1)} %write_ref.2, bf16[64,1024]{1,0:T(8,128)(2,1)} %read_ref.2, f32[12,1024]{1,0:T(8,128)} %step_ref.2, ...), custom_call_target="tpu_custom_call" | custom-call | tf_op jit(solution)/shard_map/trade/pallas_call | solution.py:510
  104.3 0.0 copy-start
  104.4 0.0 copy-done.1
  104.4 0.6 reshape.18.refs_2_
  105.0 6.8 %states_1.1 = (f32[12,64,128]{2,1,0:T(8,128)}, f32[12,128]{1,0:T(8,128)}, bf16[4,256,1536]{2,1,0:T(8,128)(2,1)}) custom-call(s32[1]{0:T(128)} %bitcast.refs_0_, f32[64,256]{1,0:T(8,128)} %get-tuple-element.16.refs_1_, f32[1,1536]{1,0:T(1,128)} %reshape.18.refs_2_, bf16[8,4,32,1536]{3,2,1,0:T(8,128)(2,1)} %get-tuple-element.17.refs_3_, ...), custom_call_target="tpu_custom_call" | custom-call | tf_op jit(solution)/shard_map/states_1/pallas_call | solution.py:496
  111.8 17.7 %prior_1.1.prior_ref = f32[12,64,128]{2,1,0:T(8,128)} custom-call(f32[12,64,128]{2,1,0:T(8,128)} %get-tuple-element.19.end_ref, f32[12,128]{1,0:T(8,128)} %get-tuple-element.20.total_ref), custom_call_target="tpu_custom_call" | custom-call | tf_op jit(solution)/shard_map/prior_1/pallas_call | solution.py:442
  129.5 0.0 copy-done
  129.5 2.3 %copy.18 = bf16[256,4,1536]{2,0,1:T(8,128)(2,1)} copy(bf16[256,4,1536]{2,1,0:T(4,128)(2,1)S(1)} %copy-done) | data formatting | bytes 6291456 | tf_op args[2]
  131.8 0.0 copy-start.2
  131.8 13.1 %main_1.1 = (f32[4,256,1536]{2,1,0:T(8,128)}, f32[8,256]{1,0:T(8,128)}) custom-call(f32[12]{0:T(128)} %skip_ref.3, bf16[4,256,1536]{2,1,0:T(8,128)(2,1)} %get-tuple-element.18.x_ref, bf16[4,256,1536]{2,1,0:T(8,128)(2,1)} %bitcast.6, bf16[64,1024]{1,0:T(8,128)(2,1)} %write_ref.3, bf16[64,1024]{1,0:T(8,128)(2,1)} %read_ref.3, f32[12,1024]{1,0:T(8,128)} %step_ref.3, ...), custom_call_target="tpu_custom_call" | custom-call | tf_op jit(solution)/shard_map/main_1/pallas_call | solution.py:511
  144.9 5.0 %squares.1.squares_ref = f32[8,256]{1,0:T(8,128)} custom-call(f32[8,256]{1,0:T(8,128)} %get-tuple-element.22.own_ref), custom_call_target="tpu_custom_call" | custom-call | tf_op jit(solution)/shard_map/squares/pallas_call | solution.py:602
  149.9 0.0 copy-done.2
  149.9 0.6 reshape.19.gain_ref
  150.5 6.7 %norm.1 = bf16[256,4,1536]{2,1,0:T(4,128)(2,1)} custom-call(f32[4,256,1536]{2,1,0:T(8,128)} %get-tuple-element.21.gated_ref, f32[8,256]{1,0:T(8,128)} %squares.1.squares_ref, f32[1,1536]{1,0:T(1,128)} %reshape.19.gain_ref), custom_call_target="tpu_custom_call" | custom-call | tf_op jit(solution)/shard_map/norm/pallas_call | solution.py:617
Async XLA Ops:
  26.8 77.6 %copy-start.1 = (f32[1536]{0:T(1024)S(1)}, f32[1536]{0:T(1024)}, u32[]{:S(2)}) copy-start(f32[1536]{0:T(1024)} %param.23) | copy-start | bytes 18436
  104.3 25.2 %copy-start = (bf16[256,4,1536]{2,1,0:T(4,128)(2,1)S(1)}, bf16[256,4,1536]{2,1,0:T(4,128)(2,1)}, u32[]{:S(2)}) copy-start(bf16[256,4,1536]{2,1,0:T(4,128)(2,1)} %param.17) | copy-start | bytes 9437188
  131.8 18.1 %copy-start.2 = (f32[1536]{0:T(1024)S(1)}, f32[1536]{0:T(1024)}, u32[]{:S(2)}) copy-start(f32[1536]{0:T(1024)} %param.29) | copy-start | bytes 18436
